TPU v7x, 32 devices: a whole 2x2x4 slice. The times are simulated.
32 devices in a mesh: quad: 4 (over z), rows: 8 (over y, x, core).
Axes of the slice: x: 2, y: 2, z: 4, core: 2. Of those that a mesh axis runs over, the one named last changes fastest.
Arguments:
- right_sides: float32 [16, 16384], P(None, 'rows'), may hold values from -36 to 36
- jacobian_tiles: float32 [1280, 128, 128], P('rows'), may hold values from -15 to 1
- row_starts: int32 [128], P('rows'), may hold values from 0 to 1279, as said below
- tile_columns: int32 [1280], P('rows'), may hold values from 0 to 127, as said below
Outputs:
- moments: float32 [8, 4, 512, 256], P('rows', 'quad')
Inputs may be any that keep to these rules, and one draw needn't show every extreme that they name: Tiles are stored by tile row in order; every tile row holds one tile or more, and its first tile is its diagonal tile. The tiles of tile rows k * 16 to (k + 1) * 16 - 1 occupy indices k * 160 to (k + 1) * 160 - 1, so row_starts[k * 16] = k * 160. `tile_columns`: A tile's column lies within 8 tile rows of its own tile row; that distance is reached.
All inputs are finite; a program needn't handle non-finite values.
Results may differ from a plain program's by a relative error of at most 0.0001.
Values sent between devices are 32-bit elements; how exact they have to be, the bound alone decides.
No kernel may reach another device: no remote copies, remote signals or barrier semaphores. Data moves between devices by JAX's collectives and lax.ppermute only.
A program may use at most 64 MiB of HBM per device.

v0:
```python
from functools import partial

import jax
import jax.numpy as jnp
import numpy as np
from jax import lax
from jax.experimental import pallas as pl
from jax.experimental.pallas import tpu as pltpu
from jax.sharding import PartitionSpec as P

MOM = 8
ITERS = 2
DEGREE = 2 * ITERS

contour_center = 3.0
contour_radius = 2.0
SHIFT = -7.0
CHUNK = 16
SPLIT_STEP = 16
GROUP = 4
highest = lax.Precision.HIGHEST
f32 = jnp.float32
bf16 = jnp.bfloat16


def vmem():
    return pl.BlockSpec(memory_space=pltpu.VMEM)


def smem():
    return pl.BlockSpec(memory_space=pltpu.SMEM)


def split_parts(value):
    high = value.astype(bf16)
    return high, (value - high.astype(f32)).astype(bf16)


def prepare_kernel(tile_rows, halo_tiles, tile_count, base_ref, starts_ref, columns_ref, tiles_ref,
                   split_ref, near_ref, far_ref, state):
    step = pl.program_id(0)
    per_step = tiles_ref.shape[0]
    size = tiles_ref.shape[1]

    @pl.when(step == 0)
    def _():
        state[0] = 0
        state[1] = 0
        state[2] = 0

    first = step * per_step
    origin = base_ref[0]
    row, near, far = state[0], state[1], state[2]
    for u in range(per_step):
        t = first + u
        following = starts_ref[jnp.minimum(row + 1, tile_rows - 1)] - starts_ref[0]
        row = row + ((row + 1 < tile_rows) & (t >= following)).astype(jnp.int32)
        column = columns_ref[t] - origin
        inside = ((column >= halo_tiles) & (column < halo_tiles + tile_rows)).astype(jnp.int32)
        entry = (t * 64 + column) * 32 + row
        near_ref[1 + near] = entry
        far_ref[1 + far] = entry
        near = near + inside
        far = far + (1 - inside)
    state[0] = row
    state[1] = near
    state[2] = far

    @pl.when(step == pl.num_programs(0) - 1)
    def _():
        near_ref[0] = near
        far_ref[0] = far
        padding = halo_tiles * 32 + tile_rows
        for u in range(CHUNK):
            near_ref[1 + near + u] = padding
            far_ref[1 + far + u] = padding

    high, low = split_parts(tiles_ref[...])
    split_ref[:, :size, :] = high
    split_ref[:, size:, :] = low


def prepare(tiles, row_starts, tile_columns, origin, tile_rows, halo_tiles):
    count, size = tiles.shape[0], tiles.shape[1]
    entries = 1 + count + CHUNK
    return pl.pallas_call(
        partial(prepare_kernel, tile_rows, halo_tiles, count),
        grid=(count // SPLIT_STEP,),
        in_specs=[smem(), smem(), smem(), pl.BlockSpec((SPLIT_STEP, size, size), lambda i: (i, 0, 0))],
        out_specs=[pl.BlockSpec((SPLIT_STEP, 2 * size, size), lambda i: (i, 0, 0)), smem(), smem()],
        out_shape=[
            jax.ShapeDtypeStruct((count, 2 * size, size), bf16),
            jax.ShapeDtypeStruct((entries,), jnp.int32),
            jax.ShapeDtypeStruct((entries,), jnp.int32),
        ],
        scratch_shapes=[pltpu.SMEM((3,), jnp.int32)],
        cost_estimate=pl.CostEstimate(flops=4 * tiles.size, bytes_accessed=8 * tiles.size, transcendentals=0),
        compiler_params=pltpu.CompilerParams(vmem_limit_bytes=12 << 20),
        name="prepare",
    )(origin, row_starts, tile_columns, tiles)


def multiply_listed(list_ref, split_ref, parts_ref, rows_ref, first_block):
    size = split_ref.shape[2]
    rhs = rows_ref.shape[1]
    rows_ref[...] = jnp.zeros_like(rows_ref)
    count = list_ref[0]

    def chunk(index, carry):
        total, last = carry
        products, owners = [], []
        for u in range(CHUNK):
            entry = list_ref[1 + index * CHUNK + u]
            row = entry & 31
            column = (entry >> 5) & 63
            tile = entry >> 11
            both = lax.dot_general(
                parts_ref[column - first_block], split_ref[tile], (((1,), (1,)), ((), ())),
                preferred_element_type=f32,
            )
            products.append((both[:rhs, :size] + both[rhs:, :size]) + (both[:rhs, size:] + both[rhs:, size:]))
            owners.append(row)
        for product, row in zip(products, owners):
            total = jnp.where(row == last, total, jnp.zeros_like(total)) + product
            rows_ref[row] = total
            last = row
        return total, last

    steps = lax.div(count + (CHUNK - 1), CHUNK)
    lax.fori_loop(0, steps, chunk, (jnp.zeros((rhs, size), f32), jnp.int32(-1)))


def store_parts(parts_ref, first, value, size):
    rhs = value.shape[0]
    high, low = split_parts(value)
    for b in range(value.shape[1] // size):
        parts_ref[first + b, :rhs, :] = high[:, b * size:(b + 1) * size]
        parts_ref[first + b, rhs:, :] = low[:, b * size:(b + 1) * size]


def near_kernel(tile_rows, halo_tiles, list_ref, split_ref, left_ref, right_ref, out_ref, parts_ref, rows_ref):
    size = split_ref.shape[2]
    half = tile_rows // 2
    store_parts(parts_ref, 0, left_ref[...], size)
    store_parts(parts_ref, half, right_ref[...], size)
    multiply_listed(list_ref, split_ref, parts_ref, rows_ref, halo_tiles)
    for r in range(tile_rows):
        source = left_ref if r < half else right_ref
        at = (r % half) * size
        out_ref[r] = rows_ref[r] - SHIFT * source[:, at:at + size]


def near_apply(entries, split, left, right, tile_rows, halo_tiles):
    rhs = left.shape[0]
    size = split.shape[2]
    return pl.pallas_call(
        partial(near_kernel, tile_rows, halo_tiles),
        in_specs=[smem(), vmem(), vmem(), vmem()],
        out_specs=vmem(),
        out_shape=jax.ShapeDtypeStruct((tile_rows, rhs, size), f32),
        scratch_shapes=[
            pltpu.VMEM((tile_rows, 2 * rhs, size), bf16),
            pltpu.VMEM((tile_rows + 1, rhs, size), f32),
        ],
        cost_estimate=pl.CostEstimate(flops=3 * split.size * rhs, bytes_accessed=2 * split.size, transcendentals=0),
        name="near",
    )(entries, split, left, right)


def far_rows(tile_rows, halo_tiles, list_ref, split_ref, low_ref, high_ref, parts_ref, rows_ref):
    size = split_ref.shape[2]
    store_parts(parts_ref, 0, low_ref[...], size)
    store_parts(parts_ref, halo_tiles + tile_rows, high_ref[...], size)
    multiply_listed(list_ref, split_ref, parts_ref, rows_ref, 0)


def far_kernel(tile_rows, halo_tiles, list_ref, split_ref, near_ref, low_ref, high_ref, left_ref, right_ref,
               parts_ref, rows_ref):
    size = split_ref.shape[2]
    half = tile_rows // 2
    far_rows(tile_rows, halo_tiles, list_ref, split_ref, low_ref, high_ref, parts_ref, rows_ref)
    for r in range(tile_rows):
        target = left_ref if r < half else right_ref
        at = (r % half) * size
        target[:, at:at + size] = near_ref[r] + rows_ref[r]


def far_scratch(split, rhs, tile_rows, halo_tiles):
    size = split.shape[2]
    return [
        pltpu.VMEM((tile_rows + 2 * halo_tiles, 2 * rhs, size), bf16),
        pltpu.VMEM((tile_rows + 1, rhs, size), f32),
    ]


def far_apply(entries, split, near, low, high, tile_rows, halo_tiles):
    rhs = low.shape[0]
    return pl.pallas_call(
        partial(far_kernel, tile_rows, halo_tiles),
        in_specs=[smem(), vmem(), vmem(), vmem(), vmem()],
        out_specs=[vmem(), vmem()],
        out_shape=[jax.ShapeDtypeStruct(low.shape, f32)] * 2,
        scratch_shapes=far_scratch(split, rhs, tile_rows, halo_tiles),
        cost_estimate=pl.CostEstimate(flops=split.size * rhs, bytes_accessed=split.size, transcendentals=0),
        name="far",
    )(entries, split, near, low, high)


def gram_kernel(tile_rows, halo_tiles, bases, out_rows, list_ref, part_ref, split_ref, near_ref, low_ref, high_ref,
                *refs):
    halves = refs[:2 * bases]
    gram_ref, slice_ref, parts_ref, rows_ref, whole_ref = refs[2 * bases:]
    size = split_ref.shape[2]
    rhs, half = low_ref.shape
    far_rows(tile_rows, halo_tiles, list_ref, split_ref, low_ref, high_ref, parts_ref, rows_ref)
    for i in range(bases):
        whole_ref[i * rhs:(i + 1) * rhs, :half] = halves[2 * i][...]
        whole_ref[i * rhs:(i + 1) * rhs, half:] = halves[2 * i + 1][...]
    for r in range(tile_rows):
        whole_ref[bases * rhs:, r * size:(r + 1) * size] = near_ref[r] + rows_ref[r]
    whole = whole_ref[...]
    gram_ref[...] = lax.dot_general(
        whole, whole, (((1,), (1,)), ((), ())), precision=highest, preferred_element_type=f32
    )
    at = pl.multiple_of(part_ref[0] * out_rows, 128)
    slice_ref[...] = whole_ref[:bases * rhs, pl.ds(at, out_rows)]


def gram_apply(entries, part, split, near, low, high, basis, tile_rows, halo_tiles, out_rows):
    rhs = low.shape[0]
    bases = len(basis) // 2
    width = (bases + 1) * rhs
    return pl.pallas_call(
        partial(gram_kernel, tile_rows, halo_tiles, bases, out_rows),
        in_specs=[smem(), smem()] + [vmem()] * (4 + len(basis)),
        out_specs=[vmem(), vmem()],
        out_shape=[
            jax.ShapeDtypeStruct((width, width), f32),
            jax.ShapeDtypeStruct((bases * rhs, out_rows), f32),
        ],
        scratch_shapes=far_scratch(split, rhs, tile_rows, halo_tiles)
        + [pltpu.VMEM((width, 2 * low.shape[1]), f32)],
        cost_estimate=pl.CostEstimate(flops=split.size * rhs, bytes_accessed=split.size, transcendentals=0),
        name="gram",
    )(entries, part, split, near, low, high, *basis)


def swapped(value):
    return pltpu.roll(value, value.shape[-1] // 2, 1)


def scaled(block, real, imaginary):
    return block * real + swapped(block) * imaginary


def stacked(blocks):
    return jnp.concatenate(blocks, axis=0)


def unstacked(value, rhs):
    return [value[i * rhs:(i + 1) * rhs] for i in range(value.shape[0] // rhs)]


def product(left, right):
    return jnp.dot(left, right, precision=highest, preferred_element_type=f32)


def solve_group(gram, zr, zi, rhs):
    lanes = 2 * GROUP * rhs
    half = lanes // 2
    lane = lax.broadcasted_iota(jnp.int32, (rhs, lanes), 1)
    line = lax.broadcasted_iota(jnp.int32, (rhs, lanes), 0)
    front = lane < half
    sign = jnp.where(lane[:1] < half, -1.0, 1.0).astype(f32)
    eye = (lane % rhs == line).astype(f32)
    tall_line = lax.broadcasted_iota(jnp.int32, (lanes, lanes), 0)
    tall_lane = lax.broadcasted_iota(jnp.int32, (lanes, lanes), 1)
    same_point = (tall_line % half) // rhs == (tall_lane % half) // rhs
    sums = same_point.astype(f32)

    def right_factor(block):
        turned = swapped(block) * sign
        return jnp.where(same_point, stacked([block] * GROUP + [turned] * GROUP), 0.0)

    def operator(blocks):
        out = [scaled(b, zr, zi) for b in blocks] + [jnp.zeros_like(blocks[0])]
        for i, b in enumerate(blocks):
            out[i + 1] = out[i + 1] - b
        return out

    def inverse(system):
        real = jnp.where(front, system, eye)
        imaginary = jnp.where(front, swapped(system), 0.0)
        origin = (lane % half) // rhs * rhs
        for p in range(rhs):
            column_r = jnp.take_along_axis(real, origin + p, axis=1)
            column_i = jnp.take_along_axis(imaginary, origin + p, axis=1)
            pivot_r, pivot_i = column_r[p:p + 1], column_i[p:p + 1]
            scale = 1.0 / (pivot_r * pivot_r + pivot_i * pivot_i)
            inverse_r, inverse_i = pivot_r * scale, -pivot_i * scale
            row_r, row_i = real[p:p + 1], imaginary[p:p + 1]
            lead_r = row_r * inverse_r - row_i * inverse_i
            lead_i = row_r * inverse_i + row_i * inverse_r
            here = line == p
            real = jnp.where(here, lead_r, real - (column_r * lead_r - column_i * lead_i))
            imaginary = jnp.where(here, lead_i, imaginary - (column_r * lead_i + column_i * lead_r))
        return jnp.where(front, swapped(real), imaginary)

    shadow = gram[:rhs]
    identity = jnp.where(front, eye, 0.0)
    direction, residual, result = [identity], [identity], []
    for iteration in range(ITERS):
        image = operator(direction)
        tall = stacked(image)
        image_gram = product(shadow[:, :tall.shape[0]], tall)
        tall_residual = stacked(residual)
        residual_gram = product(shadow[:, :tall_residual.shape[0]], tall_residual)
        solver = inverse(image_gram)
        alpha = right_factor(product(solver, right_factor(residual_gram)))
        moved = unstacked(product(stacked(image + direction), alpha), rhs)
        moved_image, moved_direction = moved[:len(image)], moved[len(image):]
        partial_block = [-m for m in moved_image]
        for i, r in enumerate(residual):
            partial_block[i] = partial_block[i] + r
        second = operator(partial_block)
        tall_second = stacked(second)
        tall_partial = stacked(partial_block + [jnp.zeros_like(identity)])
        depth = tall_second.shape[0]
        weighted = product(gram[:depth, :depth], tall_second)
        turned = swapped(weighted) * -sign
        lines = [
            jnp.sum(tall_second * weighted, axis=0, keepdims=True),
            jnp.sum(tall_partial * weighted, axis=0, keepdims=True),
            jnp.sum(tall_partial * turned, axis=0, keepdims=True),
        ]
        spread = product(stacked(lines + [jnp.zeros((5, lanes), f32)]), sums)
        inverse_norm = 1.0 / spread[0:1]
        omega_r = spread[1:2] * inverse_norm
        omega_i = -spread[2:3] * inverse_norm * sign
        step = [scaled(b, omega_r, omega_i) for b in partial_block]
        for i, m in enumerate(moved_direction):
            step[i] = step[i] + m
        for i, r in enumerate(result):
            step[i] = step[i] + r
        result = step
        if iteration + 1 < ITERS:
            residual = [-scaled(b, omega_r, omega_i) for b in second]
            for i, s in enumerate(partial_block):
                residual[i] = residual[i] + s
            beta = -product(solver, right_factor(weighted[:rhs]))
            base = [-scaled(b, omega_r, omega_i) for b in image]
            for i, d in enumerate(direction):
                base[i] = base[i] + d
            turned_base = unstacked(product(stacked(base), right_factor(beta)), rhs)
            direction = list(residual)
            for i, b in enumerate(turned_base):
                direction[i] = direction[i] + b
    return stacked(result)


def finish_kernel(rhs, groups, grams, *refs):
    gram_refs, (points_ref, table_ref, slice_ref, out_ref) = refs[:grams], refs[grams:]
    gram = gram_refs[0][...]
    for ref in gram_refs[1:]:
        gram = gram + ref[...]
    lanes = 2 * GROUP * rhs
    weights = None
    for g in range(groups):
        solved = solve_group(gram, points_ref[2 * g:2 * g + 1], points_ref[2 * g + 1:2 * g + 2], rhs)
        term = product(solved, table_ref[g * lanes:(g + 1) * lanes])
        weights = term if weights is None else weights + term
    out_ref[...] = lax.dot_general(
        slice_ref[...], weights, (((0,), (0,)), ((), ())), precision=highest, preferred_element_type=f32
    )


def contour_tables(point_count, rhs):
    groups = -(-point_count // GROUP)
    points = np.zeros((-(-2 * groups // 8) * 8, 2 * GROUP * rhs), np.float32)
    table = np.zeros((groups, 2, GROUP, rhs, 2, MOM, rhs), np.float32)
    factor = contour_radius / point_count
    powers = np.arange(1, MOM + 1)
    for j in range(groups * GROUP):
        g, slot = divmod(j, GROUP)
        angle = np.pi * (2 * min(j, point_count - 1) + 1) / point_count
        lanes = np.arange(slot * rhs, (slot + 1) * rhs)
        points[2 * g, lanes] = points[2 * g, GROUP * rhs + lanes] = contour_radius * np.cos(angle) - SHIFT
        imaginary = contour_center + contour_radius * np.sin(angle)
        points[2 * g + 1, lanes] = -imaginary
        points[2 * g + 1, GROUP * rhs + lanes] = imaginary
        if j >= point_count:
            continue
        cosine, sine = factor * np.cos(powers * angle), factor * np.sin(powers * angle)
        for c in range(rhs):
            table[g, 0, slot, c, 0, :, c] = cosine
            table[g, 0, slot, c, 1, :, c] = sine
            table[g, 1, slot, c, 0, :, c] = -sine
            table[g, 1, slot, c, 1, :, c] = cosine
    return groups, points, table.reshape(groups * 2 * GROUP * rhs, 2 * MOM * rhs)


def finish(grams, basis_slice, point_count, rhs):
    groups, points, table = contour_tables(point_count, rhs)
    return pl.pallas_call(
        partial(finish_kernel, rhs, groups, len(grams)),
        in_specs=[vmem()] * (len(grams) + 3),
        out_specs=vmem(),
        out_shape=jax.ShapeDtypeStruct((basis_slice.shape[1], table.shape[1]), f32),
        name="finish",
    )(*grams, jnp.asarray(points), jnp.asarray(table), basis_slice)


def body(right_sides, jacobian_tiles, row_starts, tile_columns):
    tile_rows = row_starts.shape[0]
    rhs = right_sides.shape[0]
    halo_tiles = tile_rows // 2
    half = right_sides.shape[1] // 2
    count = lax.axis_size("rows")
    quad_count = lax.axis_size("quad")
    forward = [(i, (i + 1) % count) for i in range(count)]
    backward = [(target, source) for source, target in forward]
    origin = (lax.axis_index("rows") * tile_rows - halo_tiles).reshape(1)
    part = lax.axis_index("quad").reshape(1)
    out_rows = right_sides.shape[1] // quad_count

    left, right = right_sides[:, :half], right_sides[:, half:]
    low = lax.ppermute(right, "rows", forward)
    high = lax.ppermute(left, "rows", backward)
    split, near_list, far_list = prepare(jacobian_tiles, row_starts, tile_columns, origin, tile_rows, halo_tiles)
    basis = []
    for power in range(DEGREE):
        if power > 0:
            low = lax.ppermute(right, "rows", forward)
            high = lax.ppermute(left, "rows", backward)
        basis += [left, right]
        near = near_apply(near_list, split, left, right, tile_rows, halo_tiles)
        if power + 1 < DEGREE:
            left, right = far_apply(far_list, split, near, low, high, tile_rows, halo_tiles)
    gram, basis_slice = gram_apply(
        far_list, part, split, near, low, high, basis, tile_rows, halo_tiles, out_rows
    )
    distance = 1
    while distance * 4 < count:
        gram = gram + lax.ppermute(gram, "rows", [(i, i ^ distance) for i in range(count)])
        distance *= 2
    grams = [gram] + [
        lax.ppermute(gram, "rows", [(i, i ^ (distance * k)) for i in range(count)])
        for k in range(1, count // distance)
    ]
    result = finish(grams, basis_slice, quad_count, rhs)
    return result.reshape(1, 1, result.shape[0], result.shape[1])


def solution(mesh):
    in_specs = (P(None, "rows"), P("rows", None, None), P("rows"), P("rows"))
    out_specs = P("rows", "quad", None, None)
    return jax.shard_map(body, mesh=mesh, in_specs=in_specs, out_specs=out_specs, check_vma=False)
```

profile of v0, /device:TPU:0, one launch (start us, length us, event | category | flops | bytes accessed | tf_op | source)
XLA Modules:
  0.0 106.6 jit_solution(2195886385921937030)
XLA Ops:
  0.0 0.9 fusion
  0.9 0.5 collective-permute-start
  1.4 2.9 %collective-permute-start.1 = (f32[16,1024]{1,0:T(8,128)S(1)}, f32[16,1024]{1,0:T(8,128)S(1)}, u32[]{:S(2)}, u32[]{:S(2)}) collective-permute-start(f32[16,1024]{1,0:T(8,128)S(1)} %get-tuple-element.28.left_ref.refs_0_), channel_id=1, source_target_pairs={{1,0},{2,1},{3,2},{4,3},{5,4},{6,5},{7,6},{0,7},{9,8},{10,9},{11,1... | collective-permute-start | bytes 196616 | tf_op jit(solution)/shard_map/ppermute | solution.py:428
  4.4 4.0 %copy-done.1 = f32[160,128,128]{2,1,0:T(8,128)S(1)} copy-done((f32[160,128,128]{2,1,0:T(8,128)S(1)}, f32[160,128,128]{2,1,0:T(8,128)}, u32[]{:S(2)}) %copy-start.1) | copy-done | bytes 10485784
  8.4 0.7 copy-done.4
  9.0 0.7 copy-done.5
  9.7 3.8 %prepare.1 = (bf16[160,256,128]{2,1,0:T(8,128)(2,1)S(1)}, s32[177]{0:T(256)S(1)}, s32[177]{0:T(256)S(1)}) custom-call(s32[1]{0:T(128)} %bitcast.base_ref, s32[16]{0:T(128)S(1)} %copy-done.5, s32[160]{0:T(256)S(1)} %copy-done.4, f32[160,128,128]{2,1,0:T(8,128)S(1)} %copy-done.1), custom_call_target="tpu_custom_call" | custom-call | flops 10485760 | bytes 20971520 | tf_op jit(solution)/shard_map/prepare/pallas_call | solution.py:86
  13.5 4.0 %copy-done = bf16[160,256,128]{2,1,0:T(8,128)(2,1)} copy-done((bf16[160,256,128]{2,1,0:T(8,128)(2,1)}, bf16[160,256,128]{2,1,0:T(8,128)(2,1)S(1)}, u32[]{:S(2)}) %copy-start) | copy-done | bytes 10485784
  17.5 0.6 copy-done.2
  18.1 0.6 copy-done.3
  18.7 8.8 %near.4.near_ref = f32[16,16,128]{2,1,0:T(8,128)} custom-call(s32[177]{0:T(256)} %copy-done.3, bf16[160,256,128]{2,1,0:T(8,128)(2,1)} %copy-done, f32[16,1024]{1,0:T(8,128)} %copy-done.7, f32[16,1024]{1,0:T(8,128)} %copy-done.6), custom_call_target="tpu_custom_call" | custom-call | flops 251658240 | bytes 10485760 | tf_op jit(solution)/shard_map/near/pallas_call | solution.py:156
  27.4 0.0 collective-permute-done.low_ref
  27.4 0.0 collective-permute-done.1.high_ref
  27.4 0.6 copy-done.10
  28.1 0.0 copy-done.12
  28.1 5.6 %far.3 = (f32[16,1024]{1,0:T(8,128)}, f32[16,1024]{1,0:T(8,128)}) custom-call(s32[177]{0:T(256)} %copy-done.2, bf16[160,256,128]{2,1,0:T(8,128)(2,1)} %copy-done, f32[16,16,128]{2,1,0:T(8,128)} %near.4.near_ref, f32[16,1024]{1,0:T(8,128)} %copy-done.10, f32[16,1024]{1,0:T(8,128)} %copy-done.12), custom_call_target="tpu_custom_call" | custom-call | flops 83886080 | bytes 5242880 | tf_op jit(solution)/shard_map/far/pallas_call | solution.py:198
  33.7 0.7 collective-permute-start.3
  34.4 0.0 collective-permute-start.2
  34.4 8.8 %near.5.near_ref = f32[16,16,128]{2,1,0:T(8,128)} custom-call(s32[177]{0:T(256)} %copy-done.3, bf16[160,256,128]{2,1,0:T(8,128)(2,1)} %copy-done, f32[16,1024]{1,0:T(8,128)} %get-tuple-element.19.left_ref.refs_2_, f32[16,1024]{1,0:T(8,128)} %get-tuple-element.20.right_ref.refs_3_), custom_call_target="tpu_custom_call" | custom-call | flops 251658240 | bytes 10485760 | tf_op jit(solution)/shard_map/near/pallas_call | solution.py:156
  43.1 0.0 collective-permute-done.3.high_ref
  43.2 0.0 collective-permute-done.2.low_ref
  43.2 0.6 copy-done.13
  43.8 0.6 copy-done.15
  44.4 5.6 %far.4 = (f32[16,1024]{1,0:T(8,128)}, f32[16,1024]{1,0:T(8,128)}) custom-call(s32[177]{0:T(256)} %copy-done.2, bf16[160,256,128]{2,1,0:T(8,128)(2,1)} %copy-done, f32[16,16,128]{2,1,0:T(8,128)} %near.5.near_ref, f32[16,1024]{1,0:T(8,128)} %copy-done.15, f32[16,1024]{1,0:T(8,128)} %copy-done.13), custom_call_target="tpu_custom_call" | custom-call | flops 83886080 | bytes 5242880 | tf_op jit(solution)/shard_map/far/pallas_call | solution.py:198
  50.1 2.6 %collective-permute-start.5 = (f32[16,1024]{1,0:T(8,128)}, f32[16,1024]{1,0:T(8,128)S(1)}, u32[]{:S(2)}, u32[]{:S(2)}) collective-permute-start(f32[16,1024]{1,0:T(8,128)} %get-tuple-element.21.left_ref.refs_4_), channel_id=1, source_target_pairs={{1,0},{2,1},{3,2},{4,3},{5,4},{6,5},{7,6},{0,7},{9,8},{10,9},{11,1... | collective-permute-start | bytes 196616 | tf_op jit(solution)/shard_map/ppermute | solution.py:434
  52.7 0.0 collective-permute-start.4
  52.7 8.8 %near.6.near_ref = f32[16,16,128]{2,1,0:T(8,128)} custom-call(s32[177]{0:T(256)} %copy-done.3, bf16[160,256,128]{2,1,0:T(8,128)(2,1)} %copy-done, f32[16,1024]{1,0:T(8,128)} %get-tuple-element.21.left_ref.refs_4_, f32[16,1024]{1,0:T(8,128)} %get-tuple-element.22.right_ref.refs_5_), custom_call_target="tpu_custom_call" | custom-call | flops 251658240 | bytes 10485760 | tf_op jit(solution)/shard_map/near/pallas_call | solution.py:156
  61.4 0.0 collective-permute-done.5.high_ref
  61.5 0.6 copy-done.14
  62.1 0.6 copy-done.16
  62.7 5.6 %far.5 = (f32[16,1024]{1,0:T(8,128)}, f32[16,1024]{1,0:T(8,128)}) custom-call(s32[177]{0:T(256)} %copy-done.2, bf16[160,256,128]{2,1,0:T(8,128)(2,1)} %copy-done, f32[16,16,128]{2,1,0:T(8,128)} %near.6.near_ref, f32[16,1024]{1,0:T(8,128)} %copy-done.16, f32[16,1024]{1,0:T(8,128)} %copy-done.14), custom_call_target="tpu_custom_call" | custom-call | flops 83886080 | bytes 5242880 | tf_op jit(solution)/shard_map/far/pallas_call | solution.py:198
  68.3 2.6 %collective-permute-start.7 = (f32[16,1024]{1,0:T(8,128)}, f32[16,1024]{1,0:T(8,128)S(1)}, u32[]{:S(2)}, u32[]{:S(2)}) collective-permute-start(f32[16,1024]{1,0:T(8,128)} %get-tuple-element.23.left_ref.refs_6_), channel_id=1, source_target_pairs={{1,0},{2,1},{3,2},{4,3},{5,4},{6,5},{7,6},{0,7},{9,8},{10,9},{11,1... | collective-permute-start | bytes 196616 | tf_op jit(solution)/shard_map/ppermute | solution.py:434
  71.0 0.0 collective-permute-start.6
  71.0 8.8 %near.7.near_ref = f32[16,16,128]{2,1,0:T(8,128)} custom-call(s32[177]{0:T(256)} %copy-done.3, bf16[160,256,128]{2,1,0:T(8,128)(2,1)} %copy-done, f32[16,1024]{1,0:T(8,128)} %get-tuple-element.23.left_ref.refs_6_, f32[16,1024]{1,0:T(8,128)} %get-tuple-element.24.right_ref.refs_7_), custom_call_target="tpu_custom_call" | custom-call | flops 251658240 | bytes 10485760 | tf_op jit(solution)/shard_map/near/pallas_call | solution.py:156
  79.8 0.0 collective-permute-done.6.low_ref
  79.8 0.6 copy-done.9
  80.4 0.0 copy-done.11
  80.4 6.4 %gram.1 = (f32[80,80]{1,0:T(8,128)}, f32[64,512]{1,0:T(8,128)}) custom-call(s32[177]{0:T(256)} %copy-done.2, s32[1]{0:T(128)} %bitcast.1.part_ref, bf16[160,256,128]{2,1,0:T(8,128)(2,1)} %copy-done, f32[16,16,128]{2,1,0:T(8,128)} %near.7.near_ref, f32[16,1024]{1,0:T(8,128)} %copy-done.11, f32[16,1024]{1,0:T(8,128)} %copy-done.9, f32[16,1024]{1,0:T(8,128)} %copy-done.7, ...), custom_call_target="tpu_custom_call" | custom-call | flops 83886080 | bytes 5242880 | tf_op jit(solution)/shard_map/gram/pallas_call | solution.py:233
  86.8 1.4 %collective-permute-done.8 = f32[80,80]{1,0:T(8,128)S(1)} collective-permute-done((f32[80,80]{1,0:T(8,128)}, f32[80,80]{1,0:T(8,128)S(1)}, u32[]{:S(2)}, u32[]{:S(2)}) %collective-permute-start.8) | collective-permute-done | bytes 25632 | tf_op jit(solution)/shard_map/ppermute | solution.py:444
  88.3 0.8 add.4.refs_0_
  89.1 2.7 %collective-permute-start.11 = (f32[80,80]{1,0:T(8,128)S(1)}, f32[80,80]{1,0:T(8,128)S(1)}, u32[]{:S(2)}, u32[]{:S(2)}) collective-permute-start(f32[80,80]{1,0:T(8,128)S(1)} %add.4.refs_0_), channel_id=1, source_target_pairs={{0,6},{1,7},{2,4},{3,5},{4,2},{5,3},{6,0},{7,1},{8,14},{9,15},{10,... | collective-permute-start | bytes 76808 | tf_op jit(solution)/shard_map/ppermute | solution.py:447
  91.7 1.5 %collective-permute-start.10 = (f32[80,80]{1,0:T(8,128)S(1)}, f32[80,80]{1,0:T(8,128)S(1)}, u32[]{:S(2)}, u32[]{:S(2)}) collective-permute-start(f32[80,80]{1,0:T(8,128)S(1)} %add.4.refs_0_), channel_id=1, source_target_pairs={{0,4},{1,5},{2,6},{3,7},{4,0},{5,1},{6,2},{7,3},{8,12},{9,13},{10,... | collective-permute-start | bytes 76808 | tf_op jit(solution)/shard_map/ppermute | solution.py:447
  93.3 0.0 collective-permute-start.9
  93.3 0.7 collective-permute-done.11.refs_3_
  94.0 1.8 %collective-permute-done.10.refs_2_ = f32[80,80]{1,0:T(8,128)S(1)} collective-permute-done((f32[80,80]{1,0:T(8,128)S(1)}, f32[80,80]{1,0:T(8,128)S(1)}, u32[]{:S(2)}, u32[]{:S(2)}) %collective-permute-start.10) | collective-permute-done | bytes 25632 | tf_op jit(solution)/shard_map/ppermute | solution.py:447
  95.7 1.5 %collective-permute-done.9.refs_1_ = f32[80,80]{1,0:T(8,128)S(1)} collective-permute-done((f32[80,80]{1,0:T(8,128)S(1)}, f32[80,80]{1,0:T(8,128)S(1)}, u32[]{:S(2)}, u32[]{:S(2)}) %collective-permute-start.9) | collective-permute-done | bytes 25632 | tf_op jit(solution)/shard_map/ppermute | solution.py:447
  97.3 0.6 copy-done.19
  97.9 8.7 %finish.1 = f32[512,256]{1,0:T(8,128)} custom-call(f32[80,80]{1,0:T(8,128)} %copy-done.8, f32[80,80]{1,0:T(8,128)} %copy-done.19, f32[80,80]{1,0:T(8,128)} %copy-done.18, f32[80,80]{1,0:T(8,128)} %copy-done.17, f32[8,128]{1,0:T(8,128)} %constant.17.clone.refs_4_, f32[128,256]{1,0:T(8,128)} %constant.18.clone.refs_5_, f32[64,512]{1,0:T(8,128)} %get-tuple-element.26.refs_6_), custom_call_target="tpu_custom_call" | custom-call | tf_op jit(solution)/shard_map/finish/pallas_call | solution.py:404
  (28 shorter events, 0.1 us)
Async XLA Ops:
  0.9 17.8 %copy-start.6 = (f32[16,1024]{1,0:T(8,128)}, f32[16,1024]{1,0:T(8,128)S(1)}, u32[]{:S(2)}) copy-start(f32[16,1024]{1,0:T(8,128)S(1)} %get-tuple-element.27.right_ref.refs_1_) | copy-start | bytes 196612
  0.9 17.8 %copy-start.7 = (f32[16,1024]{1,0:T(8,128)}, f32[16,1024]{1,0:T(8,128)S(1)}, u32[]{:S(2)}) copy-start(f32[16,1024]{1,0:T(8,128)S(1)} %get-tuple-element.28.left_ref.refs_0_) | copy-start | bytes 196612
  0.9 26.5 %collective-permute-start = (f32[16,1024]{1,0:T(8,128)S(1)}, f32[16,1024]{1,0:T(8,128)S(1)}, u32[]{:S(2)}, u32[]{:S(2)}) collective-permute-start(f32[16,1024]{1,0:T(8,128)S(1)} %get-tuple-element.27.right_ref.refs_1_), channel_id=1, source_target_pairs={{0,1},{1,2},{2,3},{3,4},{4,5},{5,6},{6,7},{7,0},{8,9},{9,10},{10,1... | collective-permute-start | bytes 196616 | tf_op jit(solution)/shard_map/ppermute | solution.py:427
  1.4 26.0 %collective-permute-start.1 = (f32[16,1024]{1,0:T(8,128)S(1)}, f32[16,1024]{1,0:T(8,128)S(1)}, u32[]{:S(2)}, u32[]{:S(2)}) collective-permute-start(f32[16,1024]{1,0:T(8,128)S(1)} %get-tuple-element.28.left_ref.refs_0_), channel_id=1, source_target_pairs={{1,0},{2,1},{3,2},{4,3},{5,4},{6,5},{7,6},{0,7},{9,8},{10,9},{11,1... | collective-permute-start | bytes 196616 | tf_op jit(solution)/shard_map/ppermute | solution.py:428
  4.4 4.0 %copy-start.1 = (f32[160,128,128]{2,1,0:T(8,128)S(1)}, f32[160,128,128]{2,1,0:T(8,128)}, u32[]{:S(2)}) copy-start(f32[160,128,128]{2,1,0:T(8,128)} %tiles_ref.1) | copy-start | bytes 31457284
  8.4 0.7 copy-start.4
  9.0 0.7 copy-start.5
  13.5 4.0 %copy-start = (bf16[160,256,128]{2,1,0:T(8,128)(2,1)}, bf16[160,256,128]{2,1,0:T(8,128)(2,1)S(1)}, u32[]{:S(2)}) copy-start(bf16[160,256,128]{2,1,0:T(8,128)(2,1)S(1)} %get-tuple-element.17.split_ref) | copy-start | bytes 31457284
  17.5 0.6 copy-start.2
  18.1 0.6 copy-start.3
  27.4 0.6 copy-start.10
  27.4 0.6 copy-start.12
  33.7 9.4 %collective-permute-start.3 = (f32[16,1024]{1,0:T(8,128)}, f32[16,1024]{1,0:T(8,128)S(1)}, u32[]{:S(2)}, u32[]{:S(2)}) collective-permute-start(f32[16,1024]{1,0:T(8,128)} %get-tuple-element.19.left_ref.refs_2_), channel_id=1, source_target_pairs={{1,0},{2,1},{3,2},{4,3},{5,4},{6,5},{7,6},{0,7},{9,8},{10,9},{11,1... | collective-permute-start | bytes 196616 | tf_op jit(solution)/shard_map/ppermute | solution.py:434
  34.4 8.8 %collective-permute-start.2 = (f32[16,1024]{1,0:T(8,128)}, f32[16,1024]{1,0:T(8,128)S(1)}, u32[]{:S(2)}, u32[]{:S(2)}) collective-permute-start(f32[16,1024]{1,0:T(8,128)} %get-tuple-element.20.right_ref.refs_3_), channel_id=1, source_target_pairs={{0,1},{1,2},{2,3},{3,4},{4,5},{5,6},{6,7},{7,0},{8,9},{9,10},{10,1... | collective-permute-start | bytes 196616 | tf_op jit(solution)/shard_map/ppermute | solution.py:433
  43.2 0.6 copy-start.13
  43.8 0.6 copy-start.15
  50.1 11.4 %collective-permute-start.5 = (f32[16,1024]{1,0:T(8,128)}, f32[16,1024]{1,0:T(8,128)S(1)}, u32[]{:S(2)}, u32[]{:S(2)}) collective-permute-start(f32[16,1024]{1,0:T(8,128)} %get-tuple-element.21.left_ref.refs_4_), channel_id=1, source_target_pairs={{1,0},{2,1},{3,2},{4,3},{5,4},{6,5},{7,6},{0,7},{9,8},{10,9},{11,1... | collective-permute-start | bytes 196616 | tf_op jit(solution)/shard_map/ppermute | solution.py:434
  52.7 8.8 %collective-permute-start.4 = (f32[16,1024]{1,0:T(8,128)}, f32[16,1024]{1,0:T(8,128)S(1)}, u32[]{:S(2)}, u32[]{:S(2)}) collective-permute-start(f32[16,1024]{1,0:T(8,128)} %get-tuple-element.22.right_ref.refs_5_), channel_id=1, source_target_pairs={{0,1},{1,2},{2,3},{3,4},{4,5},{5,6},{6,7},{7,0},{8,9},{9,10},{10,1... | collective-permute-start | bytes 196616 | tf_op jit(solution)/shard_map/ppermute | solution.py:433
  61.5 0.6 copy-start.14
  62.1 0.6 copy-start.16
  68.3 11.4 %collective-permute-start.7 = (f32[16,1024]{1,0:T(8,128)}, f32[16,1024]{1,0:T(8,128)S(1)}, u32[]{:S(2)}, u32[]{:S(2)}) collective-permute-start(f32[16,1024]{1,0:T(8,128)} %get-tuple-element.23.left_ref.refs_6_), channel_id=1, source_target_pairs={{1,0},{2,1},{3,2},{4,3},{5,4},{6,5},{7,6},{0,7},{9,8},{10,9},{11,1... | collective-permute-start | bytes 196616 | tf_op jit(solution)/shard_map/ppermute | solution.py:434
  71.0 8.8 %collective-permute-start.6 = (f32[16,1024]{1,0:T(8,128)}, f32[16,1024]{1,0:T(8,128)S(1)}, u32[]{:S(2)}, u32[]{:S(2)}) collective-permute-start(f32[16,1024]{1,0:T(8,128)} %get-tuple-element.24.right_ref.refs_7_), channel_id=1, source_target_pairs={{0,1},{1,2},{2,3},{3,4},{4,5},{5,6},{6,7},{7,0},{8,9},{9,10},{10,1... | collective-permute-start | bytes 196616 | tf_op jit(solution)/shard_map/ppermute | solution.py:433
  79.8 0.6 copy-start.9
  79.8 0.6 copy-start.11
  86.8 1.4 %collective-permute-start.8 = (f32[80,80]{1,0:T(8,128)}, f32[80,80]{1,0:T(8,128)S(1)}, u32[]{:S(2)}, u32[]{:S(2)}) collective-permute-start(f32[80,80]{1,0:T(8,128)} %get-tuple-element.25), channel_id=1, source_target_pairs={{0,1},{1,0},{2,3},{3,2},{4,5},{5,4},{6,7},{7,6},{8,9},{9,8},{10,11... | collective-permute-start | bytes 76808 | tf_op jit(solution)/shard_map/ppermute | solution.py:444
  89.1 8.2 %copy-start.8 = (f32[80,80]{1,0:T(8,128)}, f32[80,80]{1,0:T(8,128)S(1)}, u32[]{:S(2)}) copy-start(f32[80,80]{1,0:T(8,128)S(1)} %add.4.refs_0_) | copy-start | bytes 76804
  89.1 4.9 %collective-permute-start.11 = (f32[80,80]{1,0:T(8,128)S(1)}, f32[80,80]{1,0:T(8,128)S(1)}, u32[]{:S(2)}, u32[]{:S(2)}) collective-permute-start(f32[80,80]{1,0:T(8,128)S(1)} %add.4.refs_0_), channel_id=1, source_target_pairs={{0,6},{1,7},{2,4},{3,5},{4,2},{5,3},{6,0},{7,1},{8,14},{9,15},{10,... | collective-permute-start | bytes 76808 | tf_op jit(solution)/shard_map/ppermute | solution.py:447
  91.7 4.0 %collective-permute-start.10 = (f32[80,80]{1,0:T(8,128)S(1)}, f32[80,80]{1,0:T(8,128)S(1)}, u32[]{:S(2)}, u32[]{:S(2)}) collective-permute-start(f32[80,80]{1,0:T(8,128)S(1)} %add.4.refs_0_), channel_id=1, source_target_pairs={{0,4},{1,5},{2,6},{3,7},{4,0},{5,1},{6,2},{7,3},{8,12},{9,13},{10,... | collective-permute-start | bytes 76808 | tf_op jit(solution)/shard_map/ppermute | solution.py:447
  93.3 4.0 %collective-permute-start.9 = (f32[80,80]{1,0:T(8,128)S(1)}, f32[80,80]{1,0:T(8,128)S(1)}, u32[]{:S(2)}, u32[]{:S(2)}) collective-permute-start(f32[80,80]{1,0:T(8,128)S(1)} %add.4.refs_0_), channel_id=1, source_target_pairs={{0,2},{1,3},{2,0},{3,1},{4,6},{5,7},{6,4},{7,5},{8,10},{9,11},{10,... | collective-permute-start | bytes 76808 | tf_op jit(solution)/shard_map/ppermute | solution.py:447
  94.0 3.3 %copy-start.17 = (f32[80,80]{1,0:T(8,128)}, f32[80,80]{1,0:T(8,128)S(1)}, u32[]{:S(2)}) copy-start(f32[80,80]{1,0:T(8,128)S(1)} %collective-permute-done.11.refs_3_) | copy-start | bytes 76804
  95.7 1.5 %copy-start.18 = (f32[80,80]{1,0:T(8,128)}, f32[80,80]{1,0:T(8,128)S(1)}, u32[]{:S(2)}) copy-start(f32[80,80]{1,0:T(8,128)S(1)} %collective-permute-done.10.refs_2_) | copy-start | bytes 76804
  97.3 0.6 copy-start.19
where the time goes:
time: 107 us
  Pallas kernels  70.8 us (66%)
  local copies, waits for them, and re-layouts  15.8 us (15%)
  starting transfers between devices  13.7 us (13%)
  waiting for transfers between devices  5.44 us (5%)
    pallas_call x4, Pallas kernels, near_apply(): pl.pallas_call(partial(near_kernel, tile_rows, halo_tiles), in_specs=[sme...  35 us
    pallas_call x3, Pallas kernels, far_apply(): pl.pallas_call(partial(far_kernel, tile_rows, halo_tiles), in_specs=[smem...  16.9 us
    unnamed x40, local copies, waits for them, and re-layouts  14.9 us
    ppermute x4, starting transfers between devices, body(): high = lax.ppermute(left, 'rows', backward)  8.88 us
    pallas_call x1, Pallas kernels, finish(): pl.pallas_call(partial(finish_kernel, rhs, groups, len(grams)), in_specs=...  8.67 us
    pallas_call x1, Pallas kernels, gram_apply(): pl.pallas_call(partial(gram_kernel, tile_rows, halo_tiles, bases, out_row...  6.44 us
    ppermute x3, starting transfers between devices, body(): lax.ppermute(gram, 'rows', [(i, i ^ distance * k) for i in range(count)])  4.22 us
    ppermute x3, waiting for transfers between devices, body(): lax.ppermute(gram, 'rows', [(i, i ^ distance * k) for i in range(count)])  3.99 us
  transfers between devices with their start and end apart: 12, of which 4 were waited for; matrix products, arithmetic and copies ran while one was open for 0% of the time, Pallas kernels for 36%

commit v1 on v0

--- a/solution.py
+++ b/solution.py
@@ -17,6 +17,7 @@
 SHIFT = -7.0
 CHUNK = 16
 SPLIT_STEP = 16
+KERNEL_VMEM = 16 << 20
 GROUP = 4
 highest = lax.Precision.HIGHEST
 f32 = jnp.float32
@@ -36,7 +37,7 @@
     return high, (value - high.astype(f32)).astype(bf16)
 
 
-def prepare_kernel(tile_rows, halo_tiles, tile_count, base_ref, starts_ref, columns_ref, tiles_ref,
+def prepare_kernel(tile_rows, halo_tiles, quad_count, base_ref, starts_ref, columns_ref, tiles_ref,
                    split_ref, near_ref, far_ref, state):
     step = pl.program_id(0)
     per_step = tiles_ref.shape[0]
@@ -49,7 +50,7 @@
         state[2] = 0
 
     first = step * per_step
-    origin = base_ref[0]
+    origin = lax.div(base_ref[0], quad_count) * tile_rows - halo_tiles
     row, near, far = state[0], state[1], state[2]
     for u in range(per_step):
         t = first + u
@@ -80,11 +81,11 @@
     split_ref[:, size:, :] = low
 
 
-def prepare(tiles, row_starts, tile_columns, origin, tile_rows, halo_tiles):
+def prepare(tiles, row_starts, tile_columns, place, quad_count, tile_rows, halo_tiles):
     count, size = tiles.shape[0], tiles.shape[1]
     entries = 1 + count + CHUNK
     return pl.pallas_call(
-        partial(prepare_kernel, tile_rows, halo_tiles, count),
+        partial(prepare_kernel, tile_rows, halo_tiles, quad_count),
         grid=(count // SPLIT_STEP,),
         in_specs=[smem(), smem(), smem(), pl.BlockSpec((SPLIT_STEP, size, size), lambda i: (i, 0, 0))],
         out_specs=[pl.BlockSpec((SPLIT_STEP, 2 * size, size), lambda i: (i, 0, 0)), smem(), smem()],
@@ -97,7 +98,7 @@
         cost_estimate=pl.CostEstimate(flops=4 * tiles.size, bytes_accessed=8 * tiles.size, transcendentals=0),
         compiler_params=pltpu.CompilerParams(vmem_limit_bytes=12 << 20),
         name="prepare",
-    )(origin, row_starts, tile_columns, tiles)
+    )(place, row_starts, tile_columns, pltpu.with_memory_space_constraint(tiles, pltpu.HBM))
 
 
 def multiply_listed(list_ref, split_ref, parts_ref, rows_ref, first_block):
@@ -163,6 +164,7 @@
             pltpu.VMEM((tile_rows + 1, rhs, size), f32),
         ],
         cost_estimate=pl.CostEstimate(flops=3 * split.size * rhs, bytes_accessed=2 * split.size, transcendentals=0),
+        compiler_params=pltpu.CompilerParams(vmem_limit_bytes=KERNEL_VMEM),
         name="near",
     )(entries, split, left, right)
 
@@ -202,11 +204,12 @@
         out_shape=[jax.ShapeDtypeStruct(low.shape, f32)] * 2,
         scratch_shapes=far_scratch(split, rhs, tile_rows, halo_tiles),
         cost_estimate=pl.CostEstimate(flops=split.size * rhs, bytes_accessed=split.size, transcendentals=0),
+        compiler_params=pltpu.CompilerParams(vmem_limit_bytes=KERNEL_VMEM),
         name="far",
     )(entries, split, near, low, high)
 
 
-def gram_kernel(tile_rows, halo_tiles, bases, out_rows, list_ref, part_ref, split_ref, near_ref, low_ref, high_ref,
+def gram_kernel(tile_rows, halo_tiles, bases, out_rows, list_ref, place_ref, split_ref, near_ref, low_ref, high_ref,
                 *refs):
     halves = refs[:2 * bases]
     gram_ref, slice_ref, parts_ref, rows_ref, whole_ref = refs[2 * bases:]
@@ -222,11 +225,11 @@
     gram_ref[...] = lax.dot_general(
         whole, whole, (((1,), (1,)), ((), ())), precision=highest, preferred_element_type=f32
     )
-    at = pl.multiple_of(part_ref[0] * out_rows, 128)
+    at = pl.multiple_of(lax.rem(place_ref[0], whole.shape[1] // out_rows) * out_rows, 128)
     slice_ref[...] = whole_ref[:bases * rhs, pl.ds(at, out_rows)]
 
 
-def gram_apply(entries, part, split, near, low, high, basis, tile_rows, halo_tiles, out_rows):
+def gram_apply(entries, place, split, near, low, high, basis, tile_rows, halo_tiles, out_rows):
     rhs = low.shape[0]
     bases = len(basis) // 2
     width = (bases + 1) * rhs
@@ -241,8 +244,9 @@
         scratch_shapes=far_scratch(split, rhs, tile_rows, halo_tiles)
         + [pltpu.VMEM((width, 2 * low.shape[1]), f32)],
         cost_estimate=pl.CostEstimate(flops=split.size * rhs, bytes_accessed=split.size, transcendentals=0),
+        compiler_params=pltpu.CompilerParams(vmem_limit_bytes=KERNEL_VMEM),
         name="gram",
-    )(entries, part, split, near, low, high, *basis)
+    )(entries, place, split, near, low, high, *basis)
 
 
 def swapped(value):
@@ -406,6 +410,7 @@
         in_specs=[vmem()] * (len(grams) + 3),
         out_specs=vmem(),
         out_shape=jax.ShapeDtypeStruct((basis_slice.shape[1], table.shape[1]), f32),
+        compiler_params=pltpu.CompilerParams(vmem_limit_bytes=KERNEL_VMEM),
         name="finish",
     )(*grams, jnp.asarray(points), jnp.asarray(table), basis_slice)
 
@@ -419,14 +424,13 @@
     quad_count = lax.axis_size("quad")
     forward = [(i, (i + 1) % count) for i in range(count)]
     backward = [(target, source) for source, target in forward]
-    origin = (lax.axis_index("rows") * tile_rows - halo_tiles).reshape(1)
-    part = lax.axis_index("quad").reshape(1)
+    place = (lax.axis_index("rows") * quad_count + lax.axis_index("quad")).reshape(1)
     out_rows = right_sides.shape[1] // quad_count
 
     left, right = right_sides[:, :half], right_sides[:, half:]
     low = lax.ppermute(right, "rows", forward)
     high = lax.ppermute(left, "rows", backward)
-    split, near_list, far_list = prepare(jacobian_tiles, row_starts, tile_columns, origin, tile_rows, halo_tiles)
+    split, near_list, far_list = prepare(jacobian_tiles, row_starts, tile_columns, place, quad_count, tile_rows, halo_tiles)
     basis = []
     for power in range(DEGREE):
         if power > 0:
@@ -437,7 +441,7 @@
         if power + 1 < DEGREE:
             left, right = far_apply(far_list, split, near, low, high, tile_rows, halo_tiles)
     gram, basis_slice = gram_apply(
-        far_list, part, split, near, low, high, basis, tile_rows, halo_tiles, out_rows
+        far_list, place, split, near, low, high, basis, tile_rows, halo_tiles, out_rows
     )
     distance = 1
     while distance * 4 < count:

time: 107 us -> 63.3 us (0.59)
  Pallas kernels: 70.8 us -> 41.4 us
  local copies, waits for them, and re-layouts: 15.8 us -> 2.22 us
    pallas_call x4, Pallas kernels: 35 us -> 18.4 us  [near_apply(): pl.pallas_call(partial(near_kernel, tile_rows, halo_tiles), in_specs=[sme...]
    unnamed x40 -> x8, local copies, waits for them, and re-layouts: 14.9 us -> 1.34 us
    pallas_call x3, Pallas kernels: 16.9 us -> 4.45 us  [far_apply(): pl.pallas_call(partial(far_kernel, tile_rows, halo_tiles), in_specs=[smem...]
    pallas_call x1, Pallas kernels: 3.77 us -> 8.69 us  [prepare(): pl.pallas_call(partial(prepare_kernel, tile_rows, halo_tiles, quad_count)...]
    pallas_call x1, Pallas kernels: 6.44 us -> 2.22 us  [gram_apply(): pl.pallas_call(partial(gram_kernel, tile_rows, halo_tiles, bases, out_row...]
    pallas_call x1, Pallas kernels: 8.67 us -> 7.6 us  [finish(): pl.pallas_call(partial(finish_kernel, rhs, groups, len(grams)), in_specs=...]
  transfers between devices with their start and end apart: 12 -> 12, of which waited for: 4 -> 4; matrix products, arithmetic and copies ran while one was open for 0% -> 0% of each run, Pallas kernels for 36% -> 43%
where the time goes in v1:
time: 63.3 us; the launch traced here: 63 us
  Pallas kernels  41.4 us (65%)
  starting transfers between devices  14 us (22%)
  waiting for transfers between devices  5.22 us (8%)
  local copies, waits for them, and re-layouts  2.22 us (4%)
    pallas_call x4, Pallas kernels, near_apply(): pl.pallas_call(partial(near_kernel, tile_rows, halo_tiles), in_specs=[sme...  18.4 us
    ppermute x4, starting transfers between devices, body(): high = lax.ppermute(left, 'rows', backward)  9.07 us
    pallas_call x1, Pallas kernels, prepare(): pl.pallas_call(partial(prepare_kernel, tile_rows, halo_tiles, quad_count)...  8.69 us
    pallas_call x1, Pallas kernels, finish(): pl.pallas_call(partial(finish_kernel, rhs, groups, len(grams)), in_specs=...  7.6 us
    pallas_call x3, Pallas kernels, far_apply(): pl.pallas_call(partial(far_kernel, tile_rows, halo_tiles), in_specs=[smem...  4.45 us
    ppermute x3, starting transfers between devices, body(): lax.ppermute(gram, 'rows', [(i, i ^ distance * k) for i in range(count)])  4.28 us
    ppermute x3, waiting for transfers between devices, body(): lax.ppermute(gram, 'rows', [(i, i ^ distance * k) for i in range(count)])  4 us
    pallas_call x1, Pallas kernels, gram_apply(): pl.pallas_call(partial(gram_kernel, tile_rows, halo_tiles, bases, out_row...  2.22 us
  transfers between devices with their start and end apart: 12, of which 4 were waited for; matrix products, arithmetic and copies ran while one was open for 0% of the time, Pallas kernels for 43%

profile of v1, /device:TPU:0, one launch (start us, length us, event | category | flops | bytes accessed | tf_op | source)
XLA Modules:
  0.0 63.0 jit_solution(17617741981362082538)
XLA Ops:
  0.0 0.9 %fusion = (f32[16,1024]{1,0:T(8,128)S(1)}, f32[16,1024]{1,0:T(8,128)S(1)}) fusion(f32[16,2048]{1,0:T(8,128)} %param.6), kind=kLoop, calls=%fused_computation | loop fusion | bytes 262144 | tf_op jit(solution)/shard_map/slice | solution.py:430
  0.9 0.5 collective-permute-start
  1.4 2.9 %collective-permute-start.1 = (f32[16,1024]{1,0:T(8,128)S(1)}, f32[16,1024]{1,0:T(8,128)S(1)}, u32[]{:S(2)}, u32[]{:S(2)}) collective-permute-start(f32[16,1024]{1,0:T(8,128)S(1)} %get-tuple-element.28.left_ref.refs_0_), channel_id=1, source_target_pairs={{1,0},{2,1},{3,2},{4,3},{5,4},{6,5},{7,6},{0,7},{9,8},{10,9},{11,1... | collective-permute-start | bytes 196616 | tf_op jit(solution)/shard_map/ppermute | solution.py:432
  4.4 0.0 copy-start.2
  4.4 0.7 %copy-done.2 = s32[160]{0:T(256)S(1)} copy-done((s32[160]{0:T(256)S(1)}, s32[160]{0:T(256)}, u32[]{:S(2)}) %copy-start.2) | copy-done | bytes 664
  5.0 0.0 copy-start.3
  5.0 0.7 %copy-done.3 = s32[16]{0:T(128)S(1)} copy-done((s32[16]{0:T(128)S(1)}, s32[16]{0:T(128)}, u32[]{:S(2)}) %copy-start.3) | copy-done | bytes 88
  5.7 8.7 %prepare.1 = (bf16[160,256,128]{2,1,0:T(8,128)(2,1)S(1)}, s32[177]{0:T(256)S(1)}, s32[177]{0:T(256)S(1)}) custom-call(s32[1]{0:T(128)} %bitcast.base_ref.place_ref, s32[16]{0:T(128)S(1)} %copy-done.3, s32[160]{0:T(256)S(1)} %copy-done.2, f32[160,128,128]{2,1,0:T(8,128)} %tiles_ref.1), custom_call_target="tpu_custom_call" | custom-call | flops 10485760 | bytes 20971520 | tf_op jit(solution)/shard_map/prepare/pallas_call | solution.py:87
  14.4 4.6 %near.4.near_ref = f32[16,16,128]{2,1,0:T(8,128)S(1)} custom-call(s32[177]{0:T(256)S(1)} %get-tuple-element.18.list_ref, bf16[160,256,128]{2,1,0:T(8,128)(2,1)S(1)} %get-tuple-element.17.split_ref, f32[16,1024]{1,0:T(8,128)S(1)} %get-tuple-element.28.left_ref.refs_0_, f32[16,1024]{1,0:T(8,128)S(1)} %get-tuple-element.27.right_ref.refs_1_), custom_call_target="tpu_custom_call" | custom-call | flops 251658240 | bytes 10485760 | tf_op jit(solution)/shard_map/near/pallas_call | solution.py:157
  19.0 0.0 collective-permute-done.low_ref
  19.0 0.0 collective-permute-done.1.high_ref
  19.0 1.5 %far.3 = (f32[16,1024]{1,0:T(8,128)S(1)}, f32[16,1024]{1,0:T(8,128)S(1)}) custom-call(s32[177]{0:T(256)S(1)} %get-tuple-element.16.list_ref, bf16[160,256,128]{2,1,0:T(8,128)(2,1)S(1)} %get-tuple-element.17.split_ref, f32[16,16,128]{2,1,0:T(8,128)S(1)} %near.4.near_ref, f32[16,1024]{1,0:T(8,128)S(1)} %collective-permute-done.low_ref, ...), custom_call_target="tpu_custom_call" | custom-call | flops 83886080 | bytes 5242880 | tf_op jit(solution)/shard_map/far/pallas_call | solution.py:200
  20.5 0.7 %collective-permute-start.3 = (f32[16,1024]{1,0:T(8,128)S(1)}, f32[16,1024]{1,0:T(8,128)S(1)}, u32[]{:S(2)}, u32[]{:S(2)}) collective-permute-start(f32[16,1024]{1,0:T(8,128)S(1)} %get-tuple-element.19.left_ref.refs_2_), channel_id=1, source_target_pairs={{1,0},{2,1},{3,2},{4,3},{5,4},{6,5},{7,6},{0,7},{9,8},{10,9},{11,1... | collective-permute-start | bytes 196616 | tf_op jit(solution)/shard_map/ppermute | solution.py:438
  21.3 0.0 collective-permute-start.2
  21.3 4.6 %near.5.near_ref = f32[16,16,128]{2,1,0:T(8,128)S(1)} custom-call(s32[177]{0:T(256)S(1)} %get-tuple-element.18.list_ref, bf16[160,256,128]{2,1,0:T(8,128)(2,1)S(1)} %get-tuple-element.17.split_ref, f32[16,1024]{1,0:T(8,128)S(1)} %get-tuple-element.19.left_ref.refs_2_, f32[16,1024]{1,0:T(8,128)S(1)} %get-tuple-element.20.right_ref.refs_3_), custom_call_target="tpu_custom_call" | custom-call | flops 251658240 | bytes 10485760 | tf_op jit(solution)/shard_map/near/pallas_call | solution.py:157
  25.9 0.0 collective-permute-done.3.high_ref
  25.9 0.0 collective-permute-done.2.low_ref
  25.9 1.5 %far.4 = (f32[16,1024]{1,0:T(8,128)S(1)}, f32[16,1024]{1,0:T(8,128)S(1)}) custom-call(s32[177]{0:T(256)S(1)} %get-tuple-element.16.list_ref, bf16[160,256,128]{2,1,0:T(8,128)(2,1)S(1)} %get-tuple-element.17.split_ref, f32[16,16,128]{2,1,0:T(8,128)S(1)} %near.5.near_ref, f32[16,1024]{1,0:T(8,128)S(1)} %collective-permute-done.2.low_ref, ...), custom_call_target="tpu_custom_call" | custom-call | flops 83886080 | bytes 5242880 | tf_op jit(solution)/shard_map/far/pallas_call | solution.py:200
  27.4 2.7 %collective-permute-start.5 = (f32[16,1024]{1,0:T(8,128)S(1)}, f32[16,1024]{1,0:T(8,128)S(1)}, u32[]{:S(2)}, u32[]{:S(2)}) collective-permute-start(f32[16,1024]{1,0:T(8,128)S(1)} %get-tuple-element.21.left_ref.refs_4_), channel_id=1, source_target_pairs={{1,0},{2,1},{3,2},{4,3},{5,4},{6,5},{7,6},{0,7},{9,8},{10,9},{11,1... | collective-permute-start | bytes 196616 | tf_op jit(solution)/shard_map/ppermute | solution.py:438
  30.1 0.0 collective-permute-start.4
  30.1 4.6 %near.6.near_ref = f32[16,16,128]{2,1,0:T(8,128)S(1)} custom-call(s32[177]{0:T(256)S(1)} %get-tuple-element.18.list_ref, bf16[160,256,128]{2,1,0:T(8,128)(2,1)S(1)} %get-tuple-element.17.split_ref, f32[16,1024]{1,0:T(8,128)S(1)} %get-tuple-element.21.left_ref.refs_4_, f32[16,1024]{1,0:T(8,128)S(1)} %get-tuple-element.22.right_ref.refs_5_), custom_call_target="tpu_custom_call" | custom-call | flops 251658240 | bytes 10485760 | tf_op jit(solution)/shard_map/near/pallas_call | solution.py:157
  34.7 0.0 collective-permute-done.5.high_ref
  34.7 0.0 collective-permute-done.4.low_ref
  34.7 1.5 %far.5 = (f32[16,1024]{1,0:T(8,128)S(1)}, f32[16,1024]{1,0:T(8,128)S(1)}) custom-call(s32[177]{0:T(256)S(1)} %get-tuple-element.16.list_ref, bf16[160,256,128]{2,1,0:T(8,128)(2,1)S(1)} %get-tuple-element.17.split_ref, f32[16,16,128]{2,1,0:T(8,128)S(1)} %near.6.near_ref, f32[16,1024]{1,0:T(8,128)S(1)} %collective-permute-done.4.low_ref, ...), custom_call_target="tpu_custom_call" | custom-call | flops 83886080 | bytes 5242880 | tf_op jit(solution)/shard_map/far/pallas_call | solution.py:200
  36.2 2.7 %collective-permute-start.7 = (f32[16,1024]{1,0:T(8,128)S(1)}, f32[16,1024]{1,0:T(8,128)S(1)}, u32[]{:S(2)}, u32[]{:S(2)}) collective-permute-start(f32[16,1024]{1,0:T(8,128)S(1)} %get-tuple-element.23.left_ref.refs_6_), channel_id=1, source_target_pairs={{1,0},{2,1},{3,2},{4,3},{5,4},{6,5},{7,6},{0,7},{9,8},{10,9},{11,1... | collective-permute-start | bytes 196616 | tf_op jit(solution)/shard_map/ppermute | solution.py:438
  38.9 0.0 copy-start
  38.9 0.0 copy-start.1
  38.9 0.0 collective-permute-start.6
  38.9 4.6 %near.7.near_ref = f32[16,16,128]{2,1,0:T(8,128)S(1)} custom-call(s32[177]{0:T(256)S(1)} %get-tuple-element.18.list_ref, bf16[160,256,128]{2,1,0:T(8,128)(2,1)S(1)} %get-tuple-element.17.split_ref, f32[16,1024]{1,0:T(8,128)S(1)} %get-tuple-element.23.left_ref.refs_6_, f32[16,1024]{1,0:T(8,128)S(1)} %get-tuple-element.24.right_ref.refs_7_), custom_call_target="tpu_custom_call" | custom-call | flops 251658240 | bytes 10485760 | tf_op jit(solution)/shard_map/near/pallas_call | solution.py:157
  43.6 0.0 collective-permute-done.7.high_ref
  43.6 0.0 collective-permute-done.6.low_ref
  43.6 2.2 %gram.1 = (f32[80,80]{1,0:T(8,128)S(1)}, f32[64,512]{1,0:T(8,128)S(1)}) custom-call(s32[177]{0:T(256)S(1)} %get-tuple-element.16.list_ref, s32[1]{0:T(128)} %bitcast.base_ref.place_ref, bf16[160,256,128]{2,1,0:T(8,128)(2,1)S(1)} %get-tuple-element.17.split_ref, f32[16,16,128]{2,1,0:T(8,128)S(1)} %near.7.near_ref, ...), custom_call_target="tpu_custom_call" | custom-call | flops 83886080 | bytes 5242880 | tf_op jit(solution)/shard_map/gram/pallas_call | solution.py:236
  45.8 0.1 collective-permute-start.8
  45.9 1.2 %collective-permute-done.8 = f32[80,80]{1,0:T(8,128)S(1)} collective-permute-done((f32[80,80]{1,0:T(8,128)S(1)}, f32[80,80]{1,0:T(8,128)S(1)}, u32[]{:S(2)}, u32[]{:S(2)}) %collective-permute-start.8) | collective-permute-done | bytes 25632 | tf_op jit(solution)/shard_map/ppermute | solution.py:448
  47.1 2.7 %collective-permute-start.11 = (f32[80,80]{1,0:T(8,128)S(1)}, f32[80,80]{1,0:T(8,128)S(1)}, u32[]{:S(2)}, u32[]{:S(2)}) collective-permute-start(f32[80,80]{1,0:T(8,128)S(1)} %add.7.refs_0_), channel_id=1, source_target_pairs={{0,6},{1,7},{2,4},{3,5},{4,2},{5,3},{6,0},{7,1},{8,14},{9,15},{10,... | collective-permute-start | bytes 76808 | tf_op jit(solution)/shard_map/ppermute | solution.py:451
  49.8 1.6 %collective-permute-start.10 = (f32[80,80]{1,0:T(8,128)S(1)}, f32[80,80]{1,0:T(8,128)S(1)}, u32[]{:S(2)}, u32[]{:S(2)}) collective-permute-start(f32[80,80]{1,0:T(8,128)S(1)} %add.7.refs_0_), channel_id=1, source_target_pairs={{0,4},{1,5},{2,6},{3,7},{4,0},{5,1},{6,2},{7,3},{8,12},{9,13},{10,... | collective-permute-start | bytes 76808 | tf_op jit(solution)/shard_map/ppermute | solution.py:451
  51.4 0.0 collective-permute-start.9
  51.4 0.6 collective-permute-done.11.refs_3_
  52.0 1.8 %collective-permute-done.10.refs_2_ = f32[80,80]{1,0:T(8,128)S(1)} collective-permute-done((f32[80,80]{1,0:T(8,128)S(1)}, f32[80,80]{1,0:T(8,128)S(1)}, u32[]{:S(2)}, u32[]{:S(2)}) %collective-permute-start.10) | collective-permute-done | bytes 25632 | tf_op jit(solution)/shard_map/ppermute | solution.py:451
  53.8 1.6 %collective-permute-done.9.refs_1_ = f32[80,80]{1,0:T(8,128)S(1)} collective-permute-done((f32[80,80]{1,0:T(8,128)S(1)}, f32[80,80]{1,0:T(8,128)S(1)}, u32[]{:S(2)}, u32[]{:S(2)}) %collective-permute-start.9) | collective-permute-done | bytes 25632 | tf_op jit(solution)/shard_map/ppermute | solution.py:451
  55.4 0.0 copy-done
  55.4 0.0 copy-done.1
  55.4 7.6 %finish.1 = f32[512,256]{1,0:T(8,128)} custom-call(f32[80,80]{1,0:T(8,128)S(1)} %add.7.refs_0_, f32[80,80]{1,0:T(8,128)S(1)} %collective-permute-done.9.refs_1_, f32[80,80]{1,0:T(8,128)S(1)} %collective-permute-done.10.refs_2_, f32[80,80]{1,0:T(8,128)S(1)} %collective-permute-done.11.refs_3_, f32[8,128]{1,0:T(8,128)S(1)} %copy-done.1, ...), custom_call_target="tpu_custom_call" | custom-call | tf_op jit(solution)/shard_map/finish/pallas_call | solution.py:408
  (1 shorter events, 0.0 us)
Async XLA Ops:
  0.9 18.1 %collective-permute-start = (f32[16,1024]{1,0:T(8,128)S(1)}, f32[16,1024]{1,0:T(8,128)S(1)}, u32[]{:S(2)}, u32[]{:S(2)}) collective-permute-start(f32[16,1024]{1,0:T(8,128)S(1)} %get-tuple-element.27.right_ref.refs_1_), channel_id=1, source_target_pairs={{0,1},{1,2},{2,3},{3,4},{4,5},{5,6},{6,7},{7,0},{8,9},{9,10},{10,1... | collective-permute-start | bytes 196616 | tf_op jit(solution)/shard_map/ppermute | solution.py:431
  1.4 17.6 %collective-permute-start.1 = (f32[16,1024]{1,0:T(8,128)S(1)}, f32[16,1024]{1,0:T(8,128)S(1)}, u32[]{:S(2)}, u32[]{:S(2)}) collective-permute-start(f32[16,1024]{1,0:T(8,128)S(1)} %get-tuple-element.28.left_ref.refs_0_), channel_id=1, source_target_pairs={{1,0},{2,1},{3,2},{4,3},{5,4},{6,5},{7,6},{0,7},{9,8},{10,9},{11,1... | collective-permute-start | bytes 196616 | tf_op jit(solution)/shard_map/ppermute | solution.py:432
  4.4 0.7 %copy-start.2 = (s32[160]{0:T(256)S(1)}, s32[160]{0:T(256)}, u32[]{:S(2)}) copy-start(s32[160]{0:T(256)} %columns_ref.1) | copy-start | bytes 1924
  5.0 0.7 %copy-start.3 = (s32[16]{0:T(128)S(1)}, s32[16]{0:T(128)}, u32[]{:S(2)}) copy-start(s32[16]{0:T(128)} %starts_ref.1) | copy-start | bytes 196
  20.5 5.4 %collective-permute-start.3 = (f32[16,1024]{1,0:T(8,128)S(1)}, f32[16,1024]{1,0:T(8,128)S(1)}, u32[]{:S(2)}, u32[]{:S(2)}) collective-permute-start(f32[16,1024]{1,0:T(8,128)S(1)} %get-tuple-element.19.left_ref.refs_2_), channel_id=1, source_target_pairs={{1,0},{2,1},{3,2},{4,3},{5,4},{6,5},{7,6},{0,7},{9,8},{10,9},{11,1... | collective-permute-start | bytes 196616 | tf_op jit(solution)/shard_map/ppermute | solution.py:438
  21.3 4.6 %collective-permute-start.2 = (f32[16,1024]{1,0:T(8,128)S(1)}, f32[16,1024]{1,0:T(8,128)S(1)}, u32[]{:S(2)}, u32[]{:S(2)}) collective-permute-start(f32[16,1024]{1,0:T(8,128)S(1)} %get-tuple-element.20.right_ref.refs_3_), channel_id=1, source_target_pairs={{0,1},{1,2},{2,3},{3,4},{4,5},{5,6},{6,7},{7,0},{8,9},{9,10},{10,1... | collective-permute-start | bytes 196616 | tf_op jit(solution)/shard_map/ppermute | solution.py:437
  27.4 7.3 %collective-permute-start.5 = (f32[16,1024]{1,0:T(8,128)S(1)}, f32[16,1024]{1,0:T(8,128)S(1)}, u32[]{:S(2)}, u32[]{:S(2)}) collective-permute-start(f32[16,1024]{1,0:T(8,128)S(1)} %get-tuple-element.21.left_ref.refs_4_), channel_id=1, source_target_pairs={{1,0},{2,1},{3,2},{4,3},{5,4},{6,5},{7,6},{0,7},{9,8},{10,9},{11,1... | collective-permute-start | bytes 196616 | tf_op jit(solution)/shard_map/ppermute | solution.py:438
  30.1 4.6 %collective-permute-start.4 = (f32[16,1024]{1,0:T(8,128)S(1)}, f32[16,1024]{1,0:T(8,128)S(1)}, u32[]{:S(2)}, u32[]{:S(2)}) collective-permute-start(f32[16,1024]{1,0:T(8,128)S(1)} %get-tuple-element.22.right_ref.refs_5_), channel_id=1, source_target_pairs={{0,1},{1,2},{2,3},{3,4},{4,5},{5,6},{6,7},{7,0},{8,9},{9,10},{10,1... | collective-permute-start | bytes 196616 | tf_op jit(solution)/shard_map/ppermute | solution.py:437
  36.2 7.3 %collective-permute-start.7 = (f32[16,1024]{1,0:T(8,128)S(1)}, f32[16,1024]{1,0:T(8,128)S(1)}, u32[]{:S(2)}, u32[]{:S(2)}) collective-permute-start(f32[16,1024]{1,0:T(8,128)S(1)} %get-tuple-element.23.left_ref.refs_6_), channel_id=1, source_target_pairs={{1,0},{2,1},{3,2},{4,3},{5,4},{6,5},{7,6},{0,7},{9,8},{10,9},{11,1... | collective-permute-start | bytes 196616 | tf_op jit(solution)/shard_map/ppermute | solution.py:438
  38.9 16.4 %copy-start = (f32[128,256]{1,0:T(8,128)S(1)}, f32[128,256]{1,0:T(8,128)}, u32[]{:S(2)}) copy-start(f32[128,256]{1,0:T(8,128)} %constant.15.clone.refs_5_) | copy-start | bytes 393220
  38.9 16.4 %copy-start.1 = (f32[8,128]{1,0:T(8,128)S(1)}, f32[8,128]{1,0:T(8,128)}, u32[]{:S(2)}) copy-start(f32[8,128]{1,0:T(8,128)} %constant.14.clone.refs_4_) | copy-start | bytes 12292
  38.9 4.6 %collective-permute-start.6 = (f32[16,1024]{1,0:T(8,128)S(1)}, f32[16,1024]{1,0:T(8,128)S(1)}, u32[]{:S(2)}, u32[]{:S(2)}) collective-permute-start(f32[16,1024]{1,0:T(8,128)S(1)} %get-tuple-element.24.right_ref.refs_7_), channel_id=1, source_target_pairs={{0,1},{1,2},{2,3},{3,4},{4,5},{5,6},{6,7},{7,0},{8,9},{9,10},{10,1... | collective-permute-start | bytes 196616 | tf_op jit(solution)/shard_map/ppermute | solution.py:437
  45.8 1.3 %collective-permute-start.8 = (f32[80,80]{1,0:T(8,128)S(1)}, f32[80,80]{1,0:T(8,128)S(1)}, u32[]{:S(2)}, u32[]{:S(2)}) collective-permute-start(f32[80,80]{1,0:T(8,128)S(1)} %get-tuple-element.25), channel_id=1, source_target_pairs={{0,1},{1,0},{2,3},{3,2},{4,5},{5,4},{6,7},{7,6},{8,9},{9,8},{10,11... | collective-permute-start | bytes 76808 | tf_op jit(solution)/shard_map/ppermute | solution.py:448
  47.1 4.9 %collective-permute-start.11 = (f32[80,80]{1,0:T(8,128)S(1)}, f32[80,80]{1,0:T(8,128)S(1)}, u32[]{:S(2)}, u32[]{:S(2)}) collective-permute-start(f32[80,80]{1,0:T(8,128)S(1)} %add.7.refs_0_), channel_id=1, source_target_pairs={{0,6},{1,7},{2,4},{3,5},{4,2},{5,3},{6,0},{7,1},{8,14},{9,15},{10,... | collective-permute-start | bytes 76808 | tf_op jit(solution)/shard_map/ppermute | solution.py:451
  49.8 4.0 %collective-permute-start.10 = (f32[80,80]{1,0:T(8,128)S(1)}, f32[80,80]{1,0:T(8,128)S(1)}, u32[]{:S(2)}, u32[]{:S(2)}) collective-permute-start(f32[80,80]{1,0:T(8,128)S(1)} %add.7.refs_0_), channel_id=1, source_target_pairs={{0,4},{1,5},{2,6},{3,7},{4,0},{5,1},{6,2},{7,3},{8,12},{9,13},{10,... | collective-permute-start | bytes 76808 | tf_op jit(solution)/shard_map/ppermute | solution.py:451
  51.4 4.0 %collective-permute-start.9 = (f32[80,80]{1,0:T(8,128)S(1)}, f32[80,80]{1,0:T(8,128)S(1)}, u32[]{:S(2)}, u32[]{:S(2)}) collective-permute-start(f32[80,80]{1,0:T(8,128)S(1)} %add.7.refs_0_), channel_id=1, source_target_pairs={{0,2},{1,3},{2,0},{3,1},{4,6},{5,7},{6,4},{7,5},{8,10},{9,11},{10,... | collective-permute-start | bytes 76808 | tf_op jit(solution)/shard_map/ppermute | solution.py:451

commit v2 on v1

--- a/solution.py
+++ b/solution.py
@@ -15,7 +15,7 @@
 contour_center = 3.0
 contour_radius = 2.0
 SHIFT = -7.0
-CHUNK = 16
+CHUNK = 32
 SPLIT_STEP = 16
 KERNEL_VMEM = 16 << 20
 GROUP = 4
@@ -37,73 +37,118 @@
     return high, (value - high.astype(f32)).astype(bf16)
 
 
-def prepare_kernel(tile_rows, halo_tiles, quad_count, base_ref, starts_ref, columns_ref, tiles_ref,
-                   split_ref, near_ref, far_ref, state):
-    step = pl.program_id(0)
-    per_step = tiles_ref.shape[0]
-    size = tiles_ref.shape[1]
-
-    @pl.when(step == 0)
-    def _():
-        state[0] = 0
-        state[1] = 0
-        state[2] = 0
-
-    first = step * per_step
-    origin = lax.div(base_ref[0], quad_count) * tile_rows - halo_tiles
-    row, near, far = state[0], state[1], state[2]
-    for u in range(per_step):
-        t = first + u
-        following = starts_ref[jnp.minimum(row + 1, tile_rows - 1)] - starts_ref[0]
-        row = row + ((row + 1 < tile_rows) & (t >= following)).astype(jnp.int32)
-        column = columns_ref[t] - origin
-        inside = ((column >= halo_tiles) & (column < halo_tiles + tile_rows)).astype(jnp.int32)
-        entry = (t * 64 + column) * 32 + row
-        near_ref[1 + near] = entry
-        far_ref[1 + far] = entry
-        near = near + inside
-        far = far + (1 - inside)
-    state[0] = row
-    state[1] = near
-    state[2] = far
-
-    @pl.when(step == pl.num_programs(0) - 1)
-    def _():
-        near_ref[0] = near
-        far_ref[0] = far
-        padding = halo_tiles * 32 + tile_rows
-        for u in range(CHUNK):
-            near_ref[1 + near + u] = padding
-            far_ref[1 + far + u] = padding
-
-    high, low = split_parts(tiles_ref[...])
-    split_ref[:, :size, :] = high
-    split_ref[:, size:, :] = low
-
-
-def prepare(tiles, row_starts, tile_columns, place, quad_count, tile_rows, halo_tiles):
+def first_kernel(tile_rows, halo_tiles, quad_count, place_ref, starts_hbm, columns_hbm, tiles_hbm, left_ref, right_ref,
+                 split_ref, near_ref, far_ref, out_ref, tiles_ref, parts_ref, rows_ref, starts_ref, columns_ref,
+                 tile_sems, index_sems):
+    count, size = tiles_ref.shape[0], tiles_ref.shape[1]
+    rhs = left_ref.shape[0]
+    half = tile_rows // 2
+    starts_copy = pltpu.make_async_copy(starts_hbm, starts_ref, index_sems.at[0])
+    columns_copy = pltpu.make_async_copy(columns_hbm, columns_ref, index_sems.at[1])
+    starts_copy.start()
+    columns_copy.start()
+
+    def tiles_copy(step):
+        span = pl.ds(step * SPLIT_STEP, SPLIT_STEP)
+        return pltpu.make_async_copy(tiles_hbm.at[span], tiles_ref.at[span], tile_sems.at[step])
+
+    for step in range(count // SPLIT_STEP):
+        tiles_copy(step).start()
+    store_parts(parts_ref, 0, left_ref[...], size)
+    store_parts(parts_ref, half, right_ref[...], size)
+    starts_copy.wait()
+    columns_copy.wait()
+    origin = lax.div(place_ref[0], quad_count) * tile_rows - halo_tiles
+    base = starts_ref[0]
+
+    def chunk(step, carry):
+        row, near, far, total = carry
+        tiles_copy(step).wait()
+        for u in range(SPLIT_STEP):
+            t = step * SPLIT_STEP + u
+            following = starts_ref[jnp.minimum(row + 1, tile_rows - 1)] - base
+            fresh = (row + 1 < tile_rows) & (t >= following)
+            row = row + fresh.astype(jnp.int32)
+            column = columns_ref[t] - origin
+            inside = (column >= halo_tiles) & (column < halo_tiles + tile_rows)
+            entry = (t * 64 + column) * 32 + row
+            near_ref[1 + near] = entry
+            far_ref[1 + far] = entry
+            counted = inside.astype(jnp.int32)
+            near = near + counted
+            far = far + (1 - counted)
+            high, low = split_parts(tiles_ref[t].T)
+            split_ref[t, :, :size] = high
+            split_ref[t, :, size:] = low
+            local = jnp.clip(column - halo_tiles, 0, tile_rows - 1)
+            both = jnp.dot(parts_ref[local], jnp.concatenate([high, low], axis=1), preferred_element_type=f32)
+            term = (both[:rhs, :size] + both[rhs:, :size]) + (both[:rhs, size:] + both[rhs:, size:])
+            zero = jnp.zeros_like(total)
+            total = jnp.where(fresh, zero, total) + jnp.where(inside, term, zero)
+            rows_ref[row] = total
+        return row, near, far, total
+
+    zero = jnp.int32(0)
+    _, near, far, _ = lax.fori_loop(
+        0, count // SPLIT_STEP, chunk, (zero, zero, zero, jnp.zeros((rhs, size), f32))
+    )
+    near_ref[0] = near
+    far_ref[0] = far
+    padding = halo_tiles * 32 + tile_rows
+    for u in range(CHUNK):
+        near_ref[1 + near + u] = padding
+        far_ref[1 + far + u] = padding
+    shifted_rows(tile_rows, rows_ref, left_ref, right_ref, out_ref)
+
+
+def shifted_rows(tile_rows, rows_ref, left_ref, right_ref, out_ref):
+    half = tile_rows // 2
+    size = rows_ref.shape[2]
+    for r in range(tile_rows):
+        source = left_ref if r < half else right_ref
+        at = (r % half) * size
+        out_ref[r] = rows_ref[r] - SHIFT * source[:, at:at + size]
+
+
+def first_apply(tiles, row_starts, tile_columns, place, left, right, quad_count, tile_rows, halo_tiles):
     count, size = tiles.shape[0], tiles.shape[1]
+    rhs = left.shape[0]
     entries = 1 + count + CHUNK
+    hbm = pl.BlockSpec(memory_space=pl.ANY)
     return pl.pallas_call(
-        partial(prepare_kernel, tile_rows, halo_tiles, quad_count),
-        grid=(count // SPLIT_STEP,),
-        in_specs=[smem(), smem(), smem(), pl.BlockSpec((SPLIT_STEP, size, size), lambda i: (i, 0, 0))],
-        out_specs=[pl.BlockSpec((SPLIT_STEP, 2 * size, size), lambda i: (i, 0, 0)), smem(), smem()],
+        partial(first_kernel, tile_rows, halo_tiles, quad_count),
+        in_specs=[smem(), hbm, hbm, hbm, vmem(), vmem()],
+        out_specs=[vmem(), smem(), smem(), vmem()],
         out_shape=[
-            jax.ShapeDtypeStruct((count, 2 * size, size), bf16),
+            jax.ShapeDtypeStruct((count, size, 2 * size), bf16),
             jax.ShapeDtypeStruct((entries,), jnp.int32),
             jax.ShapeDtypeStruct((entries,), jnp.int32),
+            jax.ShapeDtypeStruct((tile_rows, rhs, size), f32),
         ],
-        scratch_shapes=[pltpu.SMEM((3,), jnp.int32)],
-        cost_estimate=pl.CostEstimate(flops=4 * tiles.size, bytes_accessed=8 * tiles.size, transcendentals=0),
-        compiler_params=pltpu.CompilerParams(vmem_limit_bytes=12 << 20),
-        name="prepare",
-    )(place, row_starts, tile_columns, pltpu.with_memory_space_constraint(tiles, pltpu.HBM))
+        scratch_shapes=[
+            pltpu.VMEM((count, size, size), f32),
+            pltpu.VMEM((tile_rows, 2 * rhs, size), bf16),
+            pltpu.VMEM((tile_rows, rhs, size), f32),
+            pltpu.SMEM((tile_rows,), jnp.int32),
+            pltpu.SMEM((count,), jnp.int32),
+            pltpu.SemaphoreType.DMA((count // SPLIT_STEP,)),
+            pltpu.SemaphoreType.DMA((2,)),
+        ],
+        cost_estimate=pl.CostEstimate(flops=8 * tiles.size * rhs, bytes_accessed=8 * tiles.size, transcendentals=0),
+        compiler_params=pltpu.CompilerParams(vmem_limit_bytes=24 << 20),
+        name="first",
+    )(
+        place,
+        pltpu.with_memory_space_constraint(row_starts, pltpu.HBM),
+        pltpu.with_memory_space_constraint(tile_columns, pltpu.HBM),
+        pltpu.with_memory_space_constraint(tiles, pltpu.HBM),
+        left,
+        right,
+    )
 
 
 def multiply_listed(list_ref, split_ref, parts_ref, rows_ref, first_block):
-    size = split_ref.shape[2]
-    rhs = rows_ref.shape[1]
+    rhs, size = rows_ref.shape[1:]
     rows_ref[...] = jnp.zeros_like(rows_ref)
     count = list_ref[0]
 
@@ -115,10 +160,7 @@
             row = entry & 31
             column = (entry >> 5) & 63
             tile = entry >> 11
-            both = lax.dot_general(
-                parts_ref[column - first_block], split_ref[tile], (((1,), (1,)), ((), ())),
-                preferred_element_type=f32,
-            )
+            both = jnp.dot(parts_ref[column - first_block], split_ref[tile], preferred_element_type=f32)
             products.append((both[:rhs, :size] + both[rhs:, :size]) + (both[:rhs, size:] + both[rhs:, size:]))
             owners.append(row)
         for product, row in zip(products, owners):
@@ -140,20 +182,17 @@
 
 
 def near_kernel(tile_rows, halo_tiles, list_ref, split_ref, left_ref, right_ref, out_ref, parts_ref, rows_ref):
-    size = split_ref.shape[2]
+    size = split_ref.shape[1]
     half = tile_rows // 2
     store_parts(parts_ref, 0, left_ref[...], size)
     store_parts(parts_ref, half, right_ref[...], size)
     multiply_listed(list_ref, split_ref, parts_ref, rows_ref, halo_tiles)
-    for r in range(tile_rows):
-        source = left_ref if r < half else right_ref
-        at = (r % half) * size
-        out_ref[r] = rows_ref[r] - SHIFT * source[:, at:at + size]
+    shifted_rows(tile_rows, rows_ref, left_ref, right_ref, out_ref)
 
 
 def near_apply(entries, split, left, right, tile_rows, halo_tiles):
     rhs = left.shape[0]
-    size = split.shape[2]
+    size = split.shape[1]
     return pl.pallas_call(
         partial(near_kernel, tile_rows, halo_tiles),
         in_specs=[smem(), vmem(), vmem(), vmem()],
@@ -170,7 +209,7 @@
 
 
 def far_rows(tile_rows, halo_tiles, list_ref, split_ref, low_ref, high_ref, parts_ref, rows_ref):
-    size = split_ref.shape[2]
+    size = split_ref.shape[1]
     store_parts(parts_ref, 0, low_ref[...], size)
     store_parts(parts_ref, halo_tiles + tile_rows, high_ref[...], size)
     multiply_listed(list_ref, split_ref, parts_ref, rows_ref, 0)
@@ -178,7 +217,7 @@
 
 def far_kernel(tile_rows, halo_tiles, list_ref, split_ref, near_ref, low_ref, high_ref, left_ref, right_ref,
                parts_ref, rows_ref):
-    size = split_ref.shape[2]
+    size = split_ref.shape[1]
     half = tile_rows // 2
     far_rows(tile_rows, halo_tiles, list_ref, split_ref, low_ref, high_ref, parts_ref, rows_ref)
     for r in range(tile_rows):
@@ -188,7 +227,7 @@
 
 
 def far_scratch(split, rhs, tile_rows, halo_tiles):
-    size = split.shape[2]
+    size = split.shape[1]
     return [
         pltpu.VMEM((tile_rows + 2 * halo_tiles, 2 * rhs, size), bf16),
         pltpu.VMEM((tile_rows + 1, rhs, size), f32),
@@ -213,7 +252,7 @@
                 *refs):
     halves = refs[:2 * bases]
     gram_ref, slice_ref, parts_ref, rows_ref, whole_ref = refs[2 * bases:]
-    size = split_ref.shape[2]
+    size = split_ref.shape[1]
     rhs, half = low_ref.shape
     far_rows(tile_rows, halo_tiles, list_ref, split_ref, low_ref, high_ref, parts_ref, rows_ref)
     for i in range(bases):
@@ -430,14 +469,16 @@
     left, right = right_sides[:, :half], right_sides[:, half:]
     low = lax.ppermute(right, "rows", forward)
     high = lax.ppermute(left, "rows", backward)
-    split, near_list, far_list = prepare(jacobian_tiles, row_starts, tile_columns, place, quad_count, tile_rows, halo_tiles)
+    split, near_list, far_list, near = first_apply(
+        jacobian_tiles, row_starts, tile_columns, place, left, right, quad_count, tile_rows, halo_tiles
+    )
     basis = []
     for power in range(DEGREE):
         if power > 0:
             low = lax.ppermute(right, "rows", forward)
             high = lax.ppermute(left, "rows", backward)
+            near = near_apply(near_list, split, left, right, tile_rows, halo_tiles)
         basis += [left, right]
-        near = near_apply(near_list, split, left, right, tile_rows, halo_tiles)
         if power + 1 < DEGREE:
             left, right = far_apply(far_list, split, near, low, high, tile_rows, halo_tiles)
     gram, basis_slice = gram_apply(

time: 63.3 us -> 48.7 us (0.77)
  Pallas kernels: 41.4 us -> 27.7 us
  waiting for transfers between devices: 5.22 us -> 10.5 us
  starting transfers between devices: 14 us -> 9.38 us
  local copies, waits for them, and re-layouts: 2.22 us -> 0.89 us
    pallas_call x4 -> x3, Pallas kernels: 18.4 us -> 8.1 us  [near_apply(): pl.pallas_call(partial(near_kernel, tile_rows, halo_tiles), in_specs=[sme...]
    ppermute x4, waiting for transfers between devices: 0.01 us -> 5.89 us  [body(): low = lax.ppermute(right, 'rows', forward)]
    ppermute x4, starting transfers between devices: 9.07 us -> 5 us  [body(): high = lax.ppermute(left, 'rows', backward)]
    pallas_call x3, Pallas kernels: 4.45 us -> 3.01 us  [far_apply(): pl.pallas_call(partial(far_kernel, tile_rows, halo_tiles), in_specs=[smem...]
    pallas_call x1, Pallas kernels: 8.69 us -> 7.27 us  [first_apply(): pl.pallas_call(partial(first_kernel, tile_rows, halo_tiles, quad_count),...]
    unnamed x8 -> x4, local copies, waits for them, and re-layouts: 1.34 us -> 0.01 us
  transfers between devices with their start and end apart: 12 -> 12, of which waited for: 4 -> 7; matrix products, arithmetic and copies ran while one was open for 0% -> 0% of each run, Pallas kernels for 43% -> 32%
where the time goes in v2:
time: 48.7 us; the launch traced here: 48.6 us
  Pallas kernels  27.7 us (57%)
  waiting for transfers between devices  10.5 us (22%)
  starting transfers between devices  9.38 us (19%)
  local copies, waits for them, and re-layouts  0.89 us (2%)
    pallas_call x3, Pallas kernels, near_apply(): pl.pallas_call(partial(near_kernel, tile_rows, halo_tiles), in_specs=[sme...  8.1 us
    pallas_call x1, Pallas kernels, finish(): pl.pallas_call(partial(finish_kernel, rhs, groups, len(grams)), in_specs=...  7.6 us
    pallas_call x1, Pallas kernels, first_apply(): pl.pallas_call(partial(first_kernel, tile_rows, halo_tiles, quad_count),...  7.27 us
    ppermute x4, waiting for transfers between devices, body(): low = lax.ppermute(right, 'rows', forward)  5.89 us
    ppermute x4, starting transfers between devices, body(): high = lax.ppermute(left, 'rows', backward)  5 us
    ppermute x3, starting transfers between devices, body(): lax.ppermute(gram, 'rows', [(i, i ^ distance * k) for i in range(count)])  3.69 us
    ppermute x3, waiting for transfers between devices, body(): lax.ppermute(gram, 'rows', [(i, i ^ distance * k) for i in range(count)])  3.37 us
    pallas_call x3, Pallas kernels, far_apply(): pl.pallas_call(partial(far_kernel, tile_rows, halo_tiles), in_specs=[smem...  3.01 us
  transfers between devices with their start and end apart: 12, of which 7 were waited for; matrix products, arithmetic and copies ran while one was open for 0% of the time, Pallas kernels for 32%

profile of v2, /device:TPU:0, one launch (start us, length us, event | category | flops | bytes accessed | tf_op | source)
XLA Modules:
  0.0 48.6 jit_solution(7284644581610959665)
XLA Ops:
  0.0 0.9 %fusion = (f32[16,1024]{1,0:T(8,128)S(1)}, f32[16,1024]{1,0:T(8,128)S(1)}) fusion(f32[16,2048]{1,0:T(8,128)} %param.6), kind=kLoop, calls=%fused_computation | loop fusion | bytes 262144 | tf_op jit(solution)/shard_map/slice | solution.py:469
  0.9 0.5 %collective-permute-start = (f32[16,1024]{1,0:T(8,128)S(1)}, f32[16,1024]{1,0:T(8,128)S(1)}, u32[]{:S(2)}, u32[]{:S(2)}) collective-permute-start(f32[16,1024]{1,0:T(8,128)S(1)} %get-tuple-element.29.right_ref.refs_1_), channel_id=1, source_target_pairs={{0,1},{1,2},{2,3},{3,4},{4,5},{5,6},{6,7},{7,0},{8,9},{9,10},{10,1... | collective-permute-start | bytes 196616 | tf_op jit(solution)/shard_map/ppermute | solution.py:470
  1.4 2.9 %collective-permute-start.1 = (f32[16,1024]{1,0:T(8,128)S(1)}, f32[16,1024]{1,0:T(8,128)S(1)}, u32[]{:S(2)}, u32[]{:S(2)}) collective-permute-start(f32[16,1024]{1,0:T(8,128)S(1)} %get-tuple-element.30.left_ref.refs_0_), channel_id=1, source_target_pairs={{1,0},{2,1},{3,2},{4,3},{5,4},{6,5},{7,6},{0,7},{9,8},{10,9},{11,1... | collective-permute-start | bytes 196616 | tf_op jit(solution)/shard_map/ppermute | solution.py:471
  4.4 7.3 %first.1 = (bf16[160,128,256]{2,1,0:T(8,128)(2,1)S(1)}, s32[193]{0:T(256)S(1)}, s32[193]{0:T(256)S(1)}, f32[16,16,128]{2,1,0:T(8,128)S(1)}) custom-call(s32[1]{0:T(128)} %bitcast.place_ref, s32[16]{0:T(128)} %starts_hbm.1, s32[160]{0:T(256)} %columns_hbm.1, f32[160,128,128]{2,1,0:T(8,128)} %tiles_hbm.1, f32[16,1024]{1,0:T(8,128)S(1)} %get-tuple-element.30.left_ref.refs_0_, ...), custom_call_target="tpu_custom_call" | custom-call | flops 335544320 | bytes 20971520 | tf_op jit(solution)/shard_map/first/pallas_call | solution.py:118
  11.6 0.0 collective-permute-done.low_ref
  11.7 0.0 collective-permute-done.1.high_ref
  11.7 1.0 %far.3 = (f32[16,1024]{1,0:T(8,128)S(1)}, f32[16,1024]{1,0:T(8,128)S(1)}) custom-call(s32[193]{0:T(256)S(1)} %get-tuple-element.17.list_ref, bf16[160,128,256]{2,1,0:T(8,128)(2,1)S(1)} %get-tuple-element.18.split_ref, f32[16,16,128]{2,1,0:T(8,128)S(1)} %get-tuple-element.20.near_ref, f32[16,1024]{1,0:T(8,128)S(1)} %collective-permute-done.low_ref, ...), custom_call_target="tpu_custom_call" | custom-call | flops 83886080 | bytes 5242880 | tf_op jit(solution)/shard_map/far/pallas_call | solution.py:239
  12.7 0.7 %collective-permute-start.3 = (f32[16,1024]{1,0:T(8,128)S(1)}, f32[16,1024]{1,0:T(8,128)S(1)}, u32[]{:S(2)}, u32[]{:S(2)}) collective-permute-start(f32[16,1024]{1,0:T(8,128)S(1)} %get-tuple-element.21.left_ref.refs_2_), channel_id=1, source_target_pairs={{1,0},{2,1},{3,2},{4,3},{5,4},{6,5},{7,6},{0,7},{9,8},{10,9},{11,1... | collective-permute-start | bytes 196616 | tf_op jit(solution)/shard_map/ppermute | solution.py:479
  13.4 0.0 collective-permute-start.2
  13.4 2.7 %near.3.near_ref = f32[16,16,128]{2,1,0:T(8,128)S(1)} custom-call(s32[193]{0:T(256)S(1)} %get-tuple-element.19.list_ref, bf16[160,128,256]{2,1,0:T(8,128)(2,1)S(1)} %get-tuple-element.18.split_ref, f32[16,1024]{1,0:T(8,128)S(1)} %get-tuple-element.21.left_ref.refs_2_, f32[16,1024]{1,0:T(8,128)S(1)} %get-tuple-element.22.right_ref.refs_3_), custom_call_target="tpu_custom_call" | custom-call | flops 251658240 | bytes 10485760 | tf_op jit(solution)/shard_map/near/pallas_call | solution.py:196
  16.1 0.0 collective-permute-done.3.high_ref
  16.1 2.2 %collective-permute-done.2.low_ref = f32[16,1024]{1,0:T(8,128)S(1)} collective-permute-done((f32[16,1024]{1,0:T(8,128)S(1)}, f32[16,1024]{1,0:T(8,128)S(1)}, u32[]{:S(2)}, u32[]{:S(2)}) %collective-permute-start.2) | collective-permute-done | bytes 65568 | tf_op jit(solution)/shard_map/ppermute | solution.py:478
  18.3 1.0 %far.4 = (f32[16,1024]{1,0:T(8,128)S(1)}, f32[16,1024]{1,0:T(8,128)S(1)}) custom-call(s32[193]{0:T(256)S(1)} %get-tuple-element.17.list_ref, bf16[160,128,256]{2,1,0:T(8,128)(2,1)S(1)} %get-tuple-element.18.split_ref, f32[16,16,128]{2,1,0:T(8,128)S(1)} %near.3.near_ref, f32[16,1024]{1,0:T(8,128)S(1)} %collective-permute-done.2.low_ref, ...), custom_call_target="tpu_custom_call" | custom-call | flops 83886080 | bytes 5242880 | tf_op jit(solution)/shard_map/far/pallas_call | solution.py:239
  19.4 0.5 %collective-permute-start.5 = (f32[16,1024]{1,0:T(8,128)S(1)}, f32[16,1024]{1,0:T(8,128)S(1)}, u32[]{:S(2)}, u32[]{:S(2)}) collective-permute-start(f32[16,1024]{1,0:T(8,128)S(1)} %get-tuple-element.23.left_ref.refs_4_), channel_id=1, source_target_pairs={{1,0},{2,1},{3,2},{4,3},{5,4},{6,5},{7,6},{0,7},{9,8},{10,9},{11,1... | collective-permute-start | bytes 196616 | tf_op jit(solution)/shard_map/ppermute | solution.py:479
  19.8 0.1 collective-permute-start.4
  19.9 2.7 %near.4.near_ref = f32[16,16,128]{2,1,0:T(8,128)S(1)} custom-call(s32[193]{0:T(256)S(1)} %get-tuple-element.19.list_ref, bf16[160,128,256]{2,1,0:T(8,128)(2,1)S(1)} %get-tuple-element.18.split_ref, f32[16,1024]{1,0:T(8,128)S(1)} %get-tuple-element.23.left_ref.refs_4_, f32[16,1024]{1,0:T(8,128)S(1)} %get-tuple-element.24.right_ref.refs_5_), custom_call_target="tpu_custom_call" | custom-call | flops 251658240 | bytes 10485760 | tf_op jit(solution)/shard_map/near/pallas_call | solution.py:196
  22.6 0.0 collective-permute-done.5.high_ref
  22.6 1.8 %collective-permute-done.4.low_ref = f32[16,1024]{1,0:T(8,128)S(1)} collective-permute-done((f32[16,1024]{1,0:T(8,128)S(1)}, f32[16,1024]{1,0:T(8,128)S(1)}, u32[]{:S(2)}, u32[]{:S(2)}) %collective-permute-start.4) | collective-permute-done | bytes 65568 | tf_op jit(solution)/shard_map/ppermute | solution.py:478
  24.4 1.0 %far.5 = (f32[16,1024]{1,0:T(8,128)S(1)}, f32[16,1024]{1,0:T(8,128)S(1)}) custom-call(s32[193]{0:T(256)S(1)} %get-tuple-element.17.list_ref, bf16[160,128,256]{2,1,0:T(8,128)(2,1)S(1)} %get-tuple-element.18.split_ref, f32[16,16,128]{2,1,0:T(8,128)S(1)} %near.4.near_ref, f32[16,1024]{1,0:T(8,128)S(1)} %collective-permute-done.4.low_ref, ...), custom_call_target="tpu_custom_call" | custom-call | flops 83886080 | bytes 5242880 | tf_op jit(solution)/shard_map/far/pallas_call | solution.py:239
  25.4 0.8 %collective-permute-start.7 = (f32[16,1024]{1,0:T(8,128)S(1)}, f32[16,1024]{1,0:T(8,128)S(1)}, u32[]{:S(2)}, u32[]{:S(2)}) collective-permute-start(f32[16,1024]{1,0:T(8,128)S(1)} %get-tuple-element.25.left_ref.refs_6_), channel_id=1, source_target_pairs={{1,0},{2,1},{3,2},{4,3},{5,4},{6,5},{7,6},{0,7},{9,8},{10,9},{11,1... | collective-permute-start | bytes 196616 | tf_op jit(solution)/shard_map/ppermute | solution.py:479
  26.3 0.0 copy-start
  26.3 0.0 copy-start.1
  26.3 0.0 collective-permute-start.6
  26.3 2.7 %near.5.near_ref = f32[16,16,128]{2,1,0:T(8,128)S(1)} custom-call(s32[193]{0:T(256)S(1)} %get-tuple-element.19.list_ref, bf16[160,128,256]{2,1,0:T(8,128)(2,1)S(1)} %get-tuple-element.18.split_ref, f32[16,1024]{1,0:T(8,128)S(1)} %get-tuple-element.25.left_ref.refs_6_, f32[16,1024]{1,0:T(8,128)S(1)} %get-tuple-element.26.right_ref.refs_7_), custom_call_target="tpu_custom_call" | custom-call | flops 251658240 | bytes 10485760 | tf_op jit(solution)/shard_map/near/pallas_call | solution.py:196
  29.0 0.0 collective-permute-done.7.high_ref
  29.0 1.9 %collective-permute-done.6.low_ref = f32[16,1024]{1,0:T(8,128)S(1)} collective-permute-done((f32[16,1024]{1,0:T(8,128)S(1)}, f32[16,1024]{1,0:T(8,128)S(1)}, u32[]{:S(2)}, u32[]{:S(2)}) %collective-permute-start.6) | collective-permute-done | bytes 65568 | tf_op jit(solution)/shard_map/ppermute | solution.py:478
  30.9 1.7 %gram.1 = (f32[80,80]{1,0:T(8,128)S(1)}, f32[64,512]{1,0:T(8,128)S(1)}) custom-call(s32[193]{0:T(256)S(1)} %get-tuple-element.17.list_ref, s32[1]{0:T(128)} %bitcast.place_ref, bf16[160,128,256]{2,1,0:T(8,128)(2,1)S(1)} %get-tuple-element.18.split_ref, f32[16,16,128]{2,1,0:T(8,128)S(1)} %near.5.near_ref, f32[16,1024]{1,0:T(8,128)S(1)} %collective-permute-done.6.low_ref, ...), custom_call_target="tpu_custom_call" | custom-call | flops 83886080 | bytes 5242880 | tf_op jit(solution)/shard_map/gram/pallas_call | solution.py:275
  32.6 0.1 collective-permute-start.8
  32.7 1.2 %collective-permute-done.8 = f32[80,80]{1,0:T(8,128)S(1)} collective-permute-done((f32[80,80]{1,0:T(8,128)S(1)}, f32[80,80]{1,0:T(8,128)S(1)}, u32[]{:S(2)}, u32[]{:S(2)}) %collective-permute-start.8) | collective-permute-done | bytes 25632 | tf_op jit(solution)/shard_map/ppermute | solution.py:489
  33.9 0.8 %collective-permute-start.11 = (f32[80,80]{1,0:T(8,128)S(1)}, f32[80,80]{1,0:T(8,128)S(1)}, u32[]{:S(2)}, u32[]{:S(2)}) collective-permute-start(f32[80,80]{1,0:T(8,128)S(1)} %add.7.refs_0_), channel_id=1, source_target_pairs={{0,6},{1,7},{2,4},{3,5},{4,2},{5,3},{6,0},{7,1},{8,14},{9,15},{10,... | collective-permute-start | bytes 76808 | tf_op jit(solution)/shard_map/ppermute | solution.py:492
  34.8 2.2 %collective-permute-start.10 = (f32[80,80]{1,0:T(8,128)S(1)}, f32[80,80]{1,0:T(8,128)S(1)}, u32[]{:S(2)}, u32[]{:S(2)}) collective-permute-start(f32[80,80]{1,0:T(8,128)S(1)} %add.7.refs_0_), channel_id=1, source_target_pairs={{0,4},{1,5},{2,6},{3,7},{4,0},{5,1},{6,2},{7,3},{8,12},{9,13},{10,... | collective-permute-start | bytes 76808 | tf_op jit(solution)/shard_map/ppermute | solution.py:492
  37.0 0.6 %collective-permute-start.9 = (f32[80,80]{1,0:T(8,128)S(1)}, f32[80,80]{1,0:T(8,128)S(1)}, u32[]{:S(2)}, u32[]{:S(2)}) collective-permute-start(f32[80,80]{1,0:T(8,128)S(1)} %add.7.refs_0_), channel_id=1, source_target_pairs={{0,2},{1,3},{2,0},{3,1},{4,6},{5,7},{6,4},{7,5},{8,10},{9,11},{10,... | collective-permute-start | bytes 76808 | tf_op jit(solution)/shard_map/ppermute | solution.py:492
  37.6 1.2 %collective-permute-done.11.refs_3_ = f32[80,80]{1,0:T(8,128)S(1)} collective-permute-done((f32[80,80]{1,0:T(8,128)S(1)}, f32[80,80]{1,0:T(8,128)S(1)}, u32[]{:S(2)}, u32[]{:S(2)}) %collective-permute-start.11) | collective-permute-done | bytes 25632 | tf_op jit(solution)/shard_map/ppermute | solution.py:492
  38.8 0.5 %collective-permute-done.10.refs_2_ = f32[80,80]{1,0:T(8,128)S(1)} collective-permute-done((f32[80,80]{1,0:T(8,128)S(1)}, f32[80,80]{1,0:T(8,128)S(1)}, u32[]{:S(2)}, u32[]{:S(2)}) %collective-permute-start.10) | collective-permute-done | bytes 25632 | tf_op jit(solution)/shard_map/ppermute | solution.py:492
  39.3 1.7 %collective-permute-done.9.refs_1_ = f32[80,80]{1,0:T(8,128)S(1)} collective-permute-done((f32[80,80]{1,0:T(8,128)S(1)}, f32[80,80]{1,0:T(8,128)S(1)}, u32[]{:S(2)}, u32[]{:S(2)}) %collective-permute-start.9) | collective-permute-done | bytes 25632 | tf_op jit(solution)/shard_map/ppermute | solution.py:492
  41.0 0.0 copy-done
  41.0 0.0 copy-done.1
  41.0 7.6 %finish.1 = f32[512,256]{1,0:T(8,128)} custom-call(f32[80,80]{1,0:T(8,128)S(1)} %add.7.refs_0_, f32[80,80]{1,0:T(8,128)S(1)} %collective-permute-done.9.refs_1_, f32[80,80]{1,0:T(8,128)S(1)} %collective-permute-done.10.refs_2_, f32[80,80]{1,0:T(8,128)S(1)} %collective-permute-done.11.refs_3_, f32[8,128]{1,0:T(8,128)S(1)} %copy-done.1, ...), custom_call_target="tpu_custom_call" | custom-call | tf_op jit(solution)/shard_map/finish/pallas_call | solution.py:447
  (1 shorter events, 0.0 us)
Async XLA Ops:
  0.9 10.8 %collective-permute-start = (f32[16,1024]{1,0:T(8,128)S(1)}, f32[16,1024]{1,0:T(8,128)S(1)}, u32[]{:S(2)}, u32[]{:S(2)}) collective-permute-start(f32[16,1024]{1,0:T(8,128)S(1)} %get-tuple-element.29.right_ref.refs_1_), channel_id=1, source_target_pairs={{0,1},{1,2},{2,3},{3,4},{4,5},{5,6},{6,7},{7,0},{8,9},{9,10},{10,1... | collective-permute-start | bytes 196616 | tf_op jit(solution)/shard_map/ppermute | solution.py:470
  1.4 10.2 %collective-permute-start.1 = (f32[16,1024]{1,0:T(8,128)S(1)}, f32[16,1024]{1,0:T(8,128)S(1)}, u32[]{:S(2)}, u32[]{:S(2)}) collective-permute-start(f32[16,1024]{1,0:T(8,128)S(1)} %get-tuple-element.30.left_ref.refs_0_), channel_id=1, source_target_pairs={{1,0},{2,1},{3,2},{4,3},{5,4},{6,5},{7,6},{0,7},{9,8},{10,9},{11,1... | collective-permute-start | bytes 196616 | tf_op jit(solution)/shard_map/ppermute | solution.py:471
  12.7 3.4 %collective-permute-start.3 = (f32[16,1024]{1,0:T(8,128)S(1)}, f32[16,1024]{1,0:T(8,128)S(1)}, u32[]{:S(2)}, u32[]{:S(2)}) collective-permute-start(f32[16,1024]{1,0:T(8,128)S(1)} %get-tuple-element.21.left_ref.refs_2_), channel_id=1, source_target_pairs={{1,0},{2,1},{3,2},{4,3},{5,4},{6,5},{7,6},{0,7},{9,8},{10,9},{11,1... | collective-permute-start | bytes 196616 | tf_op jit(solution)/shard_map/ppermute | solution.py:479
  13.4 4.9 %collective-permute-start.2 = (f32[16,1024]{1,0:T(8,128)S(1)}, f32[16,1024]{1,0:T(8,128)S(1)}, u32[]{:S(2)}, u32[]{:S(2)}) collective-permute-start(f32[16,1024]{1,0:T(8,128)S(1)} %get-tuple-element.22.right_ref.refs_3_), channel_id=1, source_target_pairs={{0,1},{1,2},{2,3},{3,4},{4,5},{5,6},{6,7},{7,0},{8,9},{9,10},{10,1... | collective-permute-start | bytes 196616 | tf_op jit(solution)/shard_map/ppermute | solution.py:478
  19.4 3.3 %collective-permute-start.5 = (f32[16,1024]{1,0:T(8,128)S(1)}, f32[16,1024]{1,0:T(8,128)S(1)}, u32[]{:S(2)}, u32[]{:S(2)}) collective-permute-start(f32[16,1024]{1,0:T(8,128)S(1)} %get-tuple-element.23.left_ref.refs_4_), channel_id=1, source_target_pairs={{1,0},{2,1},{3,2},{4,3},{5,4},{6,5},{7,6},{0,7},{9,8},{10,9},{11,1... | collective-permute-start | bytes 196616 | tf_op jit(solution)/shard_map/ppermute | solution.py:479
  19.8 4.6 %collective-permute-start.4 = (f32[16,1024]{1,0:T(8,128)S(1)}, f32[16,1024]{1,0:T(8,128)S(1)}, u32[]{:S(2)}, u32[]{:S(2)}) collective-permute-start(f32[16,1024]{1,0:T(8,128)S(1)} %get-tuple-element.24.right_ref.refs_5_), channel_id=1, source_target_pairs={{0,1},{1,2},{2,3},{3,4},{4,5},{5,6},{6,7},{7,0},{8,9},{9,10},{10,1... | collective-permute-start | bytes 196616 | tf_op jit(solution)/shard_map/ppermute | solution.py:478
  25.4 3.6 %collective-permute-start.7 = (f32[16,1024]{1,0:T(8,128)S(1)}, f32[16,1024]{1,0:T(8,128)S(1)}, u32[]{:S(2)}, u32[]{:S(2)}) collective-permute-start(f32[16,1024]{1,0:T(8,128)S(1)} %get-tuple-element.25.left_ref.refs_6_), channel_id=1, source_target_pairs={{1,0},{2,1},{3,2},{4,3},{5,4},{6,5},{7,6},{0,7},{9,8},{10,9},{11,1... | collective-permute-start | bytes 196616 | tf_op jit(solution)/shard_map/ppermute | solution.py:479
  26.3 14.7 %copy-start = (f32[128,256]{1,0:T(8,128)S(1)}, f32[128,256]{1,0:T(8,128)}, u32[]{:S(2)}) copy-start(f32[128,256]{1,0:T(8,128)} %constant.15.clone.refs_5_) | copy-start | bytes 393220
  26.3 14.7 %copy-start.1 = (f32[8,128]{1,0:T(8,128)S(1)}, f32[8,128]{1,0:T(8,128)}, u32[]{:S(2)}) copy-start(f32[8,128]{1,0:T(8,128)} %constant.14.clone.refs_4_) | copy-start | bytes 12292
  26.3 4.6 %collective-permute-start.6 = (f32[16,1024]{1,0:T(8,128)S(1)}, f32[16,1024]{1,0:T(8,128)S(1)}, u32[]{:S(2)}, u32[]{:S(2)}) collective-permute-start(f32[16,1024]{1,0:T(8,128)S(1)} %get-tuple-element.26.right_ref.refs_7_), channel_id=1, source_target_pairs={{0,1},{1,2},{2,3},{3,4},{4,5},{5,6},{6,7},{7,0},{8,9},{9,10},{10,1... | collective-permute-start | bytes 196616 | tf_op jit(solution)/shard_map/ppermute | solution.py:478
  32.6 1.3 %collective-permute-start.8 = (f32[80,80]{1,0:T(8,128)S(1)}, f32[80,80]{1,0:T(8,128)S(1)}, u32[]{:S(2)}, u32[]{:S(2)}) collective-permute-start(f32[80,80]{1,0:T(8,128)S(1)} %get-tuple-element.27), channel_id=1, source_target_pairs={{0,1},{1,0},{2,3},{3,2},{4,5},{5,4},{6,7},{7,6},{8,9},{9,8},{10,11... | collective-permute-start | bytes 76808 | tf_op jit(solution)/shard_map/ppermute | solution.py:489
  33.9 4.9 %collective-permute-start.11 = (f32[80,80]{1,0:T(8,128)S(1)}, f32[80,80]{1,0:T(8,128)S(1)}, u32[]{:S(2)}, u32[]{:S(2)}) collective-permute-start(f32[80,80]{1,0:T(8,128)S(1)} %add.7.refs_0_), channel_id=1, source_target_pairs={{0,6},{1,7},{2,4},{3,5},{4,2},{5,3},{6,0},{7,1},{8,14},{9,15},{10,... | collective-permute-start | bytes 76808 | tf_op jit(solution)/shard_map/ppermute | solution.py:492
  34.8 4.6 %collective-permute-start.10 = (f32[80,80]{1,0:T(8,128)S(1)}, f32[80,80]{1,0:T(8,128)S(1)}, u32[]{:S(2)}, u32[]{:S(2)}) collective-permute-start(f32[80,80]{1,0:T(8,128)S(1)} %add.7.refs_0_), channel_id=1, source_target_pairs={{0,4},{1,5},{2,6},{3,7},{4,0},{5,1},{6,2},{7,3},{8,12},{9,13},{10,... | collective-permute-start | bytes 76808 | tf_op jit(solution)/shard_map/ppermute | solution.py:492
  37.0 4.0 %collective-permute-start.9 = (f32[80,80]{1,0:T(8,128)S(1)}, f32[80,80]{1,0:T(8,128)S(1)}, u32[]{:S(2)}, u32[]{:S(2)}) collective-permute-start(f32[80,80]{1,0:T(8,128)S(1)} %add.7.refs_0_), channel_id=1, source_target_pairs={{0,2},{1,3},{2,0},{3,1},{4,6},{5,7},{6,4},{7,5},{8,10},{9,11},{10,... | collective-permute-start | bytes 76808 | tf_op jit(solution)/shard_map/ppermute | solution.py:492

commit v3 on v2

--- a/solution.py
+++ b/solution.py
@@ -15,9 +15,12 @@
 contour_center = 3.0
 contour_radius = 2.0
 SHIFT = -7.0
-CHUNK = 32
-SPLIT_STEP = 16
+SCALE = 1024.0
+NEAR_CHUNK = 32
+FAR_CHUNK = 48
+SPLIT_STEP = 32
 KERNEL_VMEM = 16 << 20
+PIVOTS = 8
 GROUP = 4
 highest = lax.Precision.HIGHEST
 f32 = jnp.float32
@@ -37,12 +40,11 @@
     return high, (value - high.astype(f32)).astype(bf16)
 
 
-def first_kernel(tile_rows, halo_tiles, quad_count, place_ref, starts_hbm, columns_hbm, tiles_hbm, left_ref, right_ref,
+def first_kernel(tile_rows, halo_tiles, quad_count, place_ref, starts_hbm, columns_hbm, tiles_hbm, block_ref,
                  split_ref, near_ref, far_ref, out_ref, tiles_ref, parts_ref, rows_ref, starts_ref, columns_ref,
                  tile_sems, index_sems):
     count, size = tiles_ref.shape[0], tiles_ref.shape[1]
-    rhs = left_ref.shape[0]
-    half = tile_rows // 2
+    rhs = block_ref.shape[0]
     starts_copy = pltpu.make_async_copy(starts_hbm, starts_ref, index_sems.at[0])
     columns_copy = pltpu.make_async_copy(columns_hbm, columns_ref, index_sems.at[1])
     starts_copy.start()
@@ -54,8 +56,7 @@
 
     for step in range(count // SPLIT_STEP):
         tiles_copy(step).start()
-    store_parts(parts_ref, 0, left_ref[...], size)
-    store_parts(parts_ref, half, right_ref[...], size)
+    store_parts(parts_ref, 0, block_ref[...], size)
     starts_copy.wait()
     columns_copy.wait()
     origin = lax.div(place_ref[0], quad_count) * tile_rows - halo_tiles
@@ -77,7 +78,8 @@
             counted = inside.astype(jnp.int32)
             near = near + counted
             far = far + (1 - counted)
-            high, low = split_parts(tiles_ref[t].T)
+            high, low = split_parts(tiles_ref[t])
+            high, low = high.T, low.T
             split_ref[t, :, :size] = high
             split_ref[t, :, size:] = low
             local = jnp.clip(column - halo_tiles, 0, tile_rows - 1)
@@ -95,34 +97,34 @@
     near_ref[0] = near
     far_ref[0] = far
     padding = halo_tiles * 32 + tile_rows
-    for u in range(CHUNK):
+    for u in range(NEAR_CHUNK):
         near_ref[1 + near + u] = padding
+    for u in range(FAR_CHUNK):
         far_ref[1 + far + u] = padding
-    shifted_rows(tile_rows, rows_ref, left_ref, right_ref, out_ref)
-
-
-def shifted_rows(tile_rows, rows_ref, left_ref, right_ref, out_ref):
-    half = tile_rows // 2
+    shifted_rows(rows_ref, [block_ref], out_ref, tile_rows)
+
+
+def shifted_rows(rows_ref, block_refs, out_ref, tile_rows):
+    per_ref = tile_rows // len(block_refs)
     size = rows_ref.shape[2]
     for r in range(tile_rows):
-        source = left_ref if r < half else right_ref
-        at = (r % half) * size
-        out_ref[r] = rows_ref[r] - SHIFT * source[:, at:at + size]
-
-
-def first_apply(tiles, row_starts, tile_columns, place, left, right, quad_count, tile_rows, halo_tiles):
+        source = block_refs[r // per_ref]
+        at = (r % per_ref) * size
+        out_ref[r] = (rows_ref[r] - SHIFT * source[:, at:at + size]) * (1.0 / SCALE)
+
+
+def first_apply(tiles, row_starts, tile_columns, place, block, quad_count, tile_rows, halo_tiles):
     count, size = tiles.shape[0], tiles.shape[1]
-    rhs = left.shape[0]
-    entries = 1 + count + CHUNK
+    rhs = block.shape[0]
     hbm = pl.BlockSpec(memory_space=pl.ANY)
     return pl.pallas_call(
         partial(first_kernel, tile_rows, halo_tiles, quad_count),
-        in_specs=[smem(), hbm, hbm, hbm, vmem(), vmem()],
+        in_specs=[smem(), hbm, hbm, hbm, vmem()],
         out_specs=[vmem(), smem(), smem(), vmem()],
         out_shape=[
             jax.ShapeDtypeStruct((count, size, 2 * size), bf16),
-            jax.ShapeDtypeStruct((entries,), jnp.int32),
-            jax.ShapeDtypeStruct((entries,), jnp.int32),
+            jax.ShapeDtypeStruct((1 + count + NEAR_CHUNK,), jnp.int32),
+            jax.ShapeDtypeStruct((1 + count + FAR_CHUNK,), jnp.int32),
             jax.ShapeDtypeStruct((tile_rows, rhs, size), f32),
         ],
         scratch_shapes=[
@@ -142,12 +144,11 @@
         pltpu.with_memory_space_constraint(row_starts, pltpu.HBM),
         pltpu.with_memory_space_constraint(tile_columns, pltpu.HBM),
         pltpu.with_memory_space_constraint(tiles, pltpu.HBM),
-        left,
-        right,
+        block,
     )
 
 
-def multiply_listed(list_ref, split_ref, parts_ref, rows_ref, first_block):
+def multiply_listed(per_step, list_ref, split_ref, parts_ref, rows_ref, first_block):
     rhs, size = rows_ref.shape[1:]
     rows_ref[...] = jnp.zeros_like(rows_ref)
     count = list_ref[0]
@@ -155,8 +156,8 @@
     def chunk(index, carry):
         total, last = carry
         products, owners = [], []
-        for u in range(CHUNK):
-            entry = list_ref[1 + index * CHUNK + u]
+        for u in range(per_step):
+            entry = list_ref[1 + index * per_step + u]
             row = entry & 31
             column = (entry >> 5) & 63
             tile = entry >> 11
@@ -169,7 +170,7 @@
             last = row
         return total, last
 
-    steps = lax.div(count + (CHUNK - 1), CHUNK)
+    steps = lax.div(count + (per_step - 1), per_step)
     lax.fori_loop(0, steps, chunk, (jnp.zeros((rhs, size), f32), jnp.int32(-1)))
 
 
@@ -186,8 +187,8 @@
     half = tile_rows // 2
     store_parts(parts_ref, 0, left_ref[...], size)
     store_parts(parts_ref, half, right_ref[...], size)
-    multiply_listed(list_ref, split_ref, parts_ref, rows_ref, halo_tiles)
-    shifted_rows(tile_rows, rows_ref, left_ref, right_ref, out_ref)
+    multiply_listed(NEAR_CHUNK, list_ref, split_ref, parts_ref, rows_ref, halo_tiles)
+    shifted_rows(rows_ref, [left_ref, right_ref], out_ref, tile_rows)
 
 
 def near_apply(entries, split, left, right, tile_rows, halo_tiles):
@@ -210,9 +211,10 @@
 
 def far_rows(tile_rows, halo_tiles, list_ref, split_ref, low_ref, high_ref, parts_ref, rows_ref):
     size = split_ref.shape[1]
-    store_parts(parts_ref, 0, low_ref[...], size)
-    store_parts(parts_ref, halo_tiles + tile_rows, high_ref[...], size)
-    multiply_listed(list_ref, split_ref, parts_ref, rows_ref, 0)
+    width = halo_tiles * size
+    store_parts(parts_ref, 0, low_ref[:, low_ref.shape[1] - width:], size)
+    store_parts(parts_ref, halo_tiles + tile_rows, high_ref[:, :width], size)
+    multiply_listed(FAR_CHUNK, list_ref, split_ref, parts_ref, rows_ref, 0)
 
 
 def far_kernel(tile_rows, halo_tiles, list_ref, split_ref, near_ref, low_ref, high_ref, left_ref, right_ref,
@@ -223,7 +225,7 @@
     for r in range(tile_rows):
         target = left_ref if r < half else right_ref
         at = (r % half) * size
-        target[:, at:at + size] = near_ref[r] + rows_ref[r]
+        target[:, at:at + size] = near_ref[r] + rows_ref[r] * (1.0 / SCALE)
 
 
 def far_scratch(split, rhs, tile_rows, halo_tiles):
@@ -240,7 +242,7 @@
         partial(far_kernel, tile_rows, halo_tiles),
         in_specs=[smem(), vmem(), vmem(), vmem(), vmem()],
         out_specs=[vmem(), vmem()],
-        out_shape=[jax.ShapeDtypeStruct(low.shape, f32)] * 2,
+        out_shape=[jax.ShapeDtypeStruct((rhs, tile_rows // 2 * split.shape[1]), f32)] * 2,
         scratch_shapes=far_scratch(split, rhs, tile_rows, halo_tiles),
         cost_estimate=pl.CostEstimate(flops=split.size * rhs, bytes_accessed=split.size, transcendentals=0),
         compiler_params=pltpu.CompilerParams(vmem_limit_bytes=KERNEL_VMEM),
@@ -250,16 +252,18 @@
 
 def gram_kernel(tile_rows, halo_tiles, bases, out_rows, list_ref, place_ref, split_ref, near_ref, low_ref, high_ref,
                 *refs):
-    halves = refs[:2 * bases]
-    gram_ref, slice_ref, parts_ref, rows_ref, whole_ref = refs[2 * bases:]
+    pieces = refs[:2 * bases - 1]
+    gram_ref, slice_ref, parts_ref, rows_ref, whole_ref = refs[2 * bases - 1:]
     size = split_ref.shape[1]
-    rhs, half = low_ref.shape
+    rhs = low_ref.shape[0]
+    half = whole_ref.shape[1] // 2
     far_rows(tile_rows, halo_tiles, list_ref, split_ref, low_ref, high_ref, parts_ref, rows_ref)
-    for i in range(bases):
-        whole_ref[i * rhs:(i + 1) * rhs, :half] = halves[2 * i][...]
-        whole_ref[i * rhs:(i + 1) * rhs, half:] = halves[2 * i + 1][...]
+    whole_ref[:rhs, :] = pieces[0][...]
+    for i in range(1, bases):
+        whole_ref[i * rhs:(i + 1) * rhs, :half] = pieces[2 * i - 1][...]
+        whole_ref[i * rhs:(i + 1) * rhs, half:] = pieces[2 * i][...]
     for r in range(tile_rows):
-        whole_ref[bases * rhs:, r * size:(r + 1) * size] = near_ref[r] + rows_ref[r]
+        whole_ref[bases * rhs:, r * size:(r + 1) * size] = near_ref[r] + rows_ref[r] * (1.0 / SCALE)
     whole = whole_ref[...]
     gram_ref[...] = lax.dot_general(
         whole, whole, (((1,), (1,)), ((), ())), precision=highest, preferred_element_type=f32
@@ -270,7 +274,7 @@
 
 def gram_apply(entries, place, split, near, low, high, basis, tile_rows, halo_tiles, out_rows):
     rhs = low.shape[0]
-    bases = len(basis) // 2
+    bases = (len(basis) + 1) // 2
     width = (bases + 1) * rhs
     return pl.pallas_call(
         partial(gram_kernel, tile_rows, halo_tiles, bases, out_rows),
@@ -281,7 +285,7 @@
             jax.ShapeDtypeStruct((bases * rhs, out_rows), f32),
         ],
         scratch_shapes=far_scratch(split, rhs, tile_rows, halo_tiles)
-        + [pltpu.VMEM((width, 2 * low.shape[1]), f32)],
+        + [pltpu.VMEM((width, basis[0].shape[1]), f32)],
         cost_estimate=pl.CostEstimate(flops=split.size * rhs, bytes_accessed=split.size, transcendentals=0),
         compiler_params=pltpu.CompilerParams(vmem_limit_bytes=KERNEL_VMEM),
         name="gram",
@@ -328,26 +332,43 @@
     def operator(blocks):
         out = [scaled(b, zr, zi) for b in blocks] + [jnp.zeros_like(blocks[0])]
         for i, b in enumerate(blocks):
-            out[i + 1] = out[i + 1] - b
+            out[i + 1] = out[i + 1] - SCALE * b
         return out
 
-    def inverse(system):
-        real = jnp.where(front, system, eye)
-        imaginary = jnp.where(front, swapped(system), 0.0)
+    def eliminate(system, known, with_inverse):
+        work = [(jnp.where(front, system, swapped(known)), jnp.where(front, swapped(system), known))]
+        if with_inverse:
+            work.append((eye, jnp.zeros_like(eye)))
         origin = (lane % half) // rhs * rhs
-        for p in range(rhs):
-            column_r = jnp.take_along_axis(real, origin + p, axis=1)
-            column_i = jnp.take_along_axis(imaginary, origin + p, axis=1)
-            pivot_r, pivot_i = column_r[p:p + 1], column_i[p:p + 1]
-            scale = 1.0 / (pivot_r * pivot_r + pivot_i * pivot_i)
-            inverse_r, inverse_i = pivot_r * scale, -pivot_i * scale
-            row_r, row_i = real[p:p + 1], imaginary[p:p + 1]
-            lead_r = row_r * inverse_r - row_i * inverse_i
-            lead_i = row_r * inverse_i + row_i * inverse_r
-            here = line == p
-            real = jnp.where(here, lead_r, real - (column_r * lead_r - column_i * lead_i))
-            imaginary = jnp.where(here, lead_i, imaginary - (column_r * lead_i + column_i * lead_r))
-        return jnp.where(front, swapped(real), imaginary)
+        for start in range(0, rhs, PIVOTS):
+            columns = [
+                tuple(jnp.take_along_axis(part, origin + p, axis=1) for part in work[0])
+                for p in range(start, start + PIVOTS)
+            ]
+            for p in range(start, start + PIVOTS):
+                here = line == p
+                column_r, column_i = columns[p - start]
+                pivot_r, pivot_i = column_r[p:p + 1], column_i[p:p + 1]
+                scale = 1.0 / (pivot_r * pivot_r + pivot_i * pivot_i)
+                inverse_r, inverse_i = pivot_r * scale, -pivot_i * scale
+
+                def reduced(pair):
+                    real, imaginary = pair
+                    row_r, row_i = real[p:p + 1], imaginary[p:p + 1]
+                    lead_r = row_r * inverse_r - row_i * inverse_i
+                    lead_i = row_r * inverse_i + row_i * inverse_r
+                    return (
+                        jnp.where(here, lead_r, real - (column_r * lead_r - column_i * lead_i)),
+                        jnp.where(here, lead_i, imaginary - (column_r * lead_i + column_i * lead_r)),
+                    )
+
+                for k in range(p - start + 1, PIVOTS):
+                    columns[k] = reduced(columns[k])
+                work = [reduced(pair) for pair in work]
+        solved = jnp.where(front, swapped(work[0][0]), work[0][1])
+        if not with_inverse:
+            return solved, None
+        return solved, jnp.where(front, work[1][0], swapped(work[1][1]))
 
     shadow = gram[:rhs]
     identity = jnp.where(front, eye, 0.0)
@@ -358,8 +379,8 @@
         image_gram = product(shadow[:, :tall.shape[0]], tall)
         tall_residual = stacked(residual)
         residual_gram = product(shadow[:, :tall_residual.shape[0]], tall_residual)
-        solver = inverse(image_gram)
-        alpha = right_factor(product(solver, right_factor(residual_gram)))
+        alpha, solver = eliminate(image_gram, residual_gram, iteration + 1 < ITERS)
+        alpha = right_factor(alpha)
         moved = unstacked(product(stacked(image + direction), alpha), rhs)
         moved_image, moved_direction = moved[:len(image)], moved[len(image):]
         partial_block = [-m for m in moved_image]
@@ -458,7 +479,6 @@
     tile_rows = row_starts.shape[0]
     rhs = right_sides.shape[0]
     halo_tiles = tile_rows // 2
-    half = right_sides.shape[1] // 2
     count = lax.axis_size("rows")
     quad_count = lax.axis_size("quad")
     forward = [(i, (i + 1) % count) for i in range(count)]
@@ -466,19 +486,18 @@
     place = (lax.axis_index("rows") * quad_count + lax.axis_index("quad")).reshape(1)
     out_rows = right_sides.shape[1] // quad_count
 
-    left, right = right_sides[:, :half], right_sides[:, half:]
-    low = lax.ppermute(right, "rows", forward)
-    high = lax.ppermute(left, "rows", backward)
+    low = lax.ppermute(right_sides, "rows", forward)
+    high = lax.ppermute(right_sides, "rows", backward)
     split, near_list, far_list, near = first_apply(
-        jacobian_tiles, row_starts, tile_columns, place, left, right, quad_count, tile_rows, halo_tiles
+        jacobian_tiles, row_starts, tile_columns, place, right_sides, quad_count, tile_rows, halo_tiles
     )
-    basis = []
+    basis = [right_sides]
     for power in range(DEGREE):
         if power > 0:
             low = lax.ppermute(right, "rows", forward)
             high = lax.ppermute(left, "rows", backward)
             near = near_apply(near_list, split, left, right, tile_rows, halo_tiles)
-        basis += [left, right]
+            basis += [left, right]
         if power + 1 < DEGREE:
             left, right = far_apply(far_list, split, near, low, high, tile_rows, halo_tiles)
     gram, basis_slice = gram_apply(

time: 48.7 us -> 44.1 us (0.906)
  Pallas kernels: 27.7 us -> 24.7 us
  waiting for transfers between devices: 10.5 us -> 9.3 us
    ppermute x0 -> x2, starting transfers between devices: none -> 3.36 us  [the longest x1 2.87 us: body(): high = lax.ppermute(right_sides, 'rows', backward)]
    ppermute x4 -> x3, starting transfers between devices: 5 us -> 1.8 us  [body(): high = lax.ppermute(left, 'rows', backward)]
    pallas_call x1, Pallas kernels: 7.6 us -> 5.13 us  [finish(): pl.pallas_call(partial(finish_kernel, rhs, groups, len(grams)), in_specs=...]
    pallas_call x1, Pallas kernels: 7.27 us -> 6.09 us  [first_apply(): pl.pallas_call(partial(first_kernel, tile_rows, halo_tiles, quad_count),...]
    ppermute x3, waiting for transfers between devices: 3.37 us -> 2.2 us  [body(): lax.ppermute(gram, 'rows', [(i, i ^ distance * k) for i in range(count)])]
    unnamed x4 -> x6, local copies, waits for them, and re-layouts: 0.01 us -> 0.94 us
    slice x1 -> x0, local copies, waits for them, and re-layouts: 0.88 us -> none  [body(): left, right = (right_sides[:, :half], right_sides[:, half:])]
    ppermute x4 -> x3, waiting for transfers between devices: 5.89 us -> 5.89 us  [body(): low = lax.ppermute(right, 'rows', forward)]
where the time goes in v3:
time: 44.1 us
  Pallas kernels  24.7 us (56%)
  waiting for transfers between devices  9.3 us (21%)
  starting transfers between devices  9.03 us (20%)
  local copies, waits for them, and re-layouts  0.94 us (2%)
    pallas_call x3, Pallas kernels, near_apply(): pl.pallas_call(partial(near_kernel, tile_rows, halo_tiles), in_specs=[sme...  8.12 us
    pallas_call x1, Pallas kernels, first_apply(): pl.pallas_call(partial(first_kernel, tile_rows, halo_tiles, quad_count),...  6.09 us
    ppermute x3, waiting for transfers between devices, body(): low = lax.ppermute(right, 'rows', forward)  5.89 us
    pallas_call x1, Pallas kernels, finish(): pl.pallas_call(partial(finish_kernel, rhs, groups, len(grams)), in_specs=...  5.13 us
    ppermute x3, starting transfers between devices, body(): lax.ppermute(gram, 'rows', [(i, i ^ distance * k) for i in range(count)])  3.49 us
    pallas_call x3, Pallas kernels, far_apply(): pl.pallas_call(partial(far_kernel, tile_rows, halo_tiles), in_specs=[smem...  3.45 us
    ppermute x1, starting transfers between devices, body(): high = lax.ppermute(right_sides, 'rows', backward)  2.87 us
    ppermute x3, waiting for transfers between devices, body(): lax.ppermute(gram, 'rows', [(i, i ^ distance * k) for i in range(count)])  2.2 us
  transfers between devices with their start and end apart: 12, of which 7 were waited for; matrix products, arithmetic and copies ran while one was open for 0% of the time, Pallas kernels for 32%

profile of v3, /device:TPU:0, one launch (start us, length us, event | category | flops | bytes accessed | tf_op | source)
XLA Modules:
  0.0 44.1 jit_solution(12245065961438229535)
XLA Ops:
  0.0 0.5 %collective-permute-start = (f32[16,2048]{1,0:T(8,128)}, f32[16,2048]{1,0:T(8,128)S(1)}, u32[]{:S(2)}, u32[]{:S(2)}) collective-permute-start(f32[16,2048]{1,0:T(8,128)} %refs_0_.1), channel_id=1, source_target_pairs={{0,1},{1,2},{2,3},{3,4},{4,5},{5,6},{6,7},{7,0},{8,9},{9,10},{10,1... | collective-permute-start | bytes 393224 | tf_op jit(solution)/shard_map/ppermute | solution.py:489
  0.5 2.9 %collective-permute-start.1 = (f32[16,2048]{1,0:T(8,128)}, f32[16,2048]{1,0:T(8,128)S(1)}, u32[]{:S(2)}, u32[]{:S(2)}) collective-permute-start(f32[16,2048]{1,0:T(8,128)} %refs_0_.1), channel_id=1, source_target_pairs={{1,0},{2,1},{3,2},{4,3},{5,4},{6,5},{7,6},{0,7},{9,8},{10,9},{11,1... | collective-permute-start | bytes 393224 | tf_op jit(solution)/shard_map/ppermute | solution.py:490
  3.4 0.0 copy-start
  3.4 0.9 %copy-done = f32[16,2048]{1,0:T(8,128)S(1)} copy-done((f32[16,2048]{1,0:T(8,128)S(1)}, f32[16,2048]{1,0:T(8,128)}, u32[]{:S(2)}) %copy-start) | copy-done | bytes 131096
  4.3 6.1 %first.1 = (bf16[160,128,256]{2,1,0:T(8,128)(2,1)S(1)}, s32[193]{0:T(256)S(1)}, s32[209]{0:T(256)S(1)}, f32[16,16,128]{2,1,0:T(8,128)S(1)}) custom-call(s32[1]{0:T(128)} %bitcast.place_ref, s32[16]{0:T(128)} %starts_hbm.1, s32[160]{0:T(256)} %columns_hbm.1, f32[160,128,128]{2,1,0:T(8,128)} %tiles_hbm.1, f32[16,2048]{1,0:T(8,128)S(1)} %copy-done), custom_call_target="tpu_custom_call" | custom-call | flops 335544320 | bytes 20971520 | tf_op jit(solution)/shard_map/first/pallas_call | solution.py:120
  10.4 0.0 collective-permute-done.low_ref
  10.4 0.0 collective-permute-done.1.high_ref
  10.4 1.2 %far.3 = (f32[16,1024]{1,0:T(8,128)S(1)}, f32[16,1024]{1,0:T(8,128)S(1)}) custom-call(s32[209]{0:T(256)S(1)} %get-tuple-element.17.list_ref, bf16[160,128,256]{2,1,0:T(8,128)(2,1)S(1)} %get-tuple-element.18.split_ref, f32[16,16,128]{2,1,0:T(8,128)S(1)} %get-tuple-element.20.near_ref, f32[16,2048]{1,0:T(8,128)S(1)} %collective-permute-done.low_ref, ...), custom_call_target="tpu_custom_call" | custom-call | flops 83886080 | bytes 5242880 | tf_op jit(solution)/shard_map/far/pallas_call | solution.py:241
  11.6 0.7 %collective-permute-start.3 = (f32[16,1024]{1,0:T(8,128)S(1)}, f32[16,1024]{1,0:T(8,128)S(1)}, u32[]{:S(2)}, u32[]{:S(2)}) collective-permute-start(f32[16,1024]{1,0:T(8,128)S(1)} %get-tuple-element.21.left_ref.refs_1_), channel_id=1, source_target_pairs={{1,0},{2,1},{3,2},{4,3},{5,4},{6,5},{7,6},{0,7},{9,8},{10,9},{11,1... | collective-permute-start | bytes 196616 | tf_op jit(solution)/shard_map/ppermute | solution.py:498
  12.3 0.0 collective-permute-start.2
  12.3 2.7 %near.3.near_ref = f32[16,16,128]{2,1,0:T(8,128)S(1)} custom-call(s32[193]{0:T(256)S(1)} %get-tuple-element.19.list_ref, bf16[160,128,256]{2,1,0:T(8,128)(2,1)S(1)} %get-tuple-element.18.split_ref, f32[16,1024]{1,0:T(8,128)S(1)} %get-tuple-element.21.left_ref.refs_1_, f32[16,1024]{1,0:T(8,128)S(1)} %get-tuple-element.22.right_ref.refs_2_), custom_call_target="tpu_custom_call" | custom-call | flops 251658240 | bytes 10485760 | tf_op jit(solution)/shard_map/near/pallas_call | solution.py:197
  15.0 0.0 collective-permute-done.3.high_ref
  15.0 2.5 %collective-permute-done.2.low_ref = f32[16,1024]{1,0:T(8,128)S(1)} collective-permute-done((f32[16,1024]{1,0:T(8,128)S(1)}, f32[16,1024]{1,0:T(8,128)S(1)}, u32[]{:S(2)}, u32[]{:S(2)}) %collective-permute-start.2) | collective-permute-done | bytes 65568 | tf_op jit(solution)/shard_map/ppermute | solution.py:497
  17.5 1.1 %far.4 = (f32[16,1024]{1,0:T(8,128)S(1)}, f32[16,1024]{1,0:T(8,128)S(1)}) custom-call(s32[209]{0:T(256)S(1)} %get-tuple-element.17.list_ref, bf16[160,128,256]{2,1,0:T(8,128)(2,1)S(1)} %get-tuple-element.18.split_ref, f32[16,16,128]{2,1,0:T(8,128)S(1)} %near.3.near_ref, f32[16,1024]{1,0:T(8,128)S(1)} %collective-permute-done.2.low_ref, ...), custom_call_target="tpu_custom_call" | custom-call | flops 83886080 | bytes 5242880 | tf_op jit(solution)/shard_map/far/pallas_call | solution.py:241
  18.6 0.3 collective-permute-start.5
  18.9 0.3 collective-permute-start.4
  19.2 2.7 %near.4.near_ref = f32[16,16,128]{2,1,0:T(8,128)S(1)} custom-call(s32[193]{0:T(256)S(1)} %get-tuple-element.19.list_ref, bf16[160,128,256]{2,1,0:T(8,128)(2,1)S(1)} %get-tuple-element.18.split_ref, f32[16,1024]{1,0:T(8,128)S(1)} %get-tuple-element.23.left_ref.refs_3_, f32[16,1024]{1,0:T(8,128)S(1)} %get-tuple-element.24.right_ref.refs_4_), custom_call_target="tpu_custom_call" | custom-call | flops 251658240 | bytes 10485760 | tf_op jit(solution)/shard_map/near/pallas_call | solution.py:197
  21.9 0.0 collective-permute-done.5.high_ref
  21.9 1.6 %collective-permute-done.4.low_ref = f32[16,1024]{1,0:T(8,128)S(1)} collective-permute-done((f32[16,1024]{1,0:T(8,128)S(1)}, f32[16,1024]{1,0:T(8,128)S(1)}, u32[]{:S(2)}, u32[]{:S(2)}) %collective-permute-start.4) | collective-permute-done | bytes 65568 | tf_op jit(solution)/shard_map/ppermute | solution.py:497
  23.5 1.1 %far.5 = (f32[16,1024]{1,0:T(8,128)S(1)}, f32[16,1024]{1,0:T(8,128)S(1)}) custom-call(s32[209]{0:T(256)S(1)} %get-tuple-element.17.list_ref, bf16[160,128,256]{2,1,0:T(8,128)(2,1)S(1)} %get-tuple-element.18.split_ref, f32[16,16,128]{2,1,0:T(8,128)S(1)} %near.4.near_ref, f32[16,1024]{1,0:T(8,128)S(1)} %collective-permute-done.4.low_ref, ...), custom_call_target="tpu_custom_call" | custom-call | flops 83886080 | bytes 5242880 | tf_op jit(solution)/shard_map/far/pallas_call | solution.py:241
  24.6 0.8 %collective-permute-start.7 = (f32[16,1024]{1,0:T(8,128)S(1)}, f32[16,1024]{1,0:T(8,128)S(1)}, u32[]{:S(2)}, u32[]{:S(2)}) collective-permute-start(f32[16,1024]{1,0:T(8,128)S(1)} %get-tuple-element.25.left_ref.refs_5_), channel_id=1, source_target_pairs={{1,0},{2,1},{3,2},{4,3},{5,4},{6,5},{7,6},{0,7},{9,8},{10,9},{11,1... | collective-permute-start | bytes 196616 | tf_op jit(solution)/shard_map/ppermute | solution.py:498
  25.5 0.0 copy-start.1
  25.5 0.0 copy-start.2
  25.5 0.0 collective-permute-start.6
  25.5 2.7 %near.5.near_ref = f32[16,16,128]{2,1,0:T(8,128)S(1)} custom-call(s32[193]{0:T(256)S(1)} %get-tuple-element.19.list_ref, bf16[160,128,256]{2,1,0:T(8,128)(2,1)S(1)} %get-tuple-element.18.split_ref, f32[16,1024]{1,0:T(8,128)S(1)} %get-tuple-element.25.left_ref.refs_5_, f32[16,1024]{1,0:T(8,128)S(1)} %get-tuple-element.26.right_ref.refs_6_), custom_call_target="tpu_custom_call" | custom-call | flops 251658240 | bytes 10485760 | tf_op jit(solution)/shard_map/near/pallas_call | solution.py:197
  28.2 0.0 collective-permute-done.7.high_ref
  28.2 1.9 %collective-permute-done.6.low_ref = f32[16,1024]{1,0:T(8,128)S(1)} collective-permute-done((f32[16,1024]{1,0:T(8,128)S(1)}, f32[16,1024]{1,0:T(8,128)S(1)}, u32[]{:S(2)}, u32[]{:S(2)}) %collective-permute-start.6) | collective-permute-done | bytes 65568 | tf_op jit(solution)/shard_map/ppermute | solution.py:497
  30.1 1.9 %gram.1 = (f32[80,80]{1,0:T(8,128)S(1)}, f32[64,512]{1,0:T(8,128)S(1)}) custom-call(s32[209]{0:T(256)S(1)} %get-tuple-element.17.list_ref, s32[1]{0:T(128)} %bitcast.place_ref, bf16[160,128,256]{2,1,0:T(8,128)(2,1)S(1)} %get-tuple-element.18.split_ref, f32[16,16,128]{2,1,0:T(8,128)S(1)} %near.5.near_ref, f32[16,1024]{1,0:T(8,128)S(1)} %collective-permute-done.6.low_ref, ...), custom_call_target="tpu_custom_call" | custom-call | flops 83886080 | bytes 5242880 | tf_op jit(solution)/shard_map/gram/pallas_call | solution.py:279
  31.9 0.1 collective-permute-start.8
  32.0 1.2 %collective-permute-done.8 = f32[80,80]{1,0:T(8,128)S(1)} collective-permute-done((f32[80,80]{1,0:T(8,128)S(1)}, f32[80,80]{1,0:T(8,128)S(1)}, u32[]{:S(2)}, u32[]{:S(2)}) %collective-permute-start.8) | collective-permute-done | bytes 25632 | tf_op jit(solution)/shard_map/ppermute | solution.py:508
  33.2 1.2 %collective-permute-start.11 = (f32[80,80]{1,0:T(8,128)S(1)}, f32[80,80]{1,0:T(8,128)S(1)}, u32[]{:S(2)}, u32[]{:S(2)}) collective-permute-start(f32[80,80]{1,0:T(8,128)S(1)} %add.7.refs_0_), channel_id=1, source_target_pairs={{0,6},{1,7},{2,4},{3,5},{4,2},{5,3},{6,0},{7,1},{8,14},{9,15},{10,... | collective-permute-start | bytes 76808 | tf_op jit(solution)/shard_map/ppermute | solution.py:511
  34.5 0.5 %collective-permute-start.10 = (f32[80,80]{1,0:T(8,128)S(1)}, f32[80,80]{1,0:T(8,128)S(1)}, u32[]{:S(2)}, u32[]{:S(2)}) collective-permute-start(f32[80,80]{1,0:T(8,128)S(1)} %add.7.refs_0_), channel_id=1, source_target_pairs={{0,4},{1,5},{2,6},{3,7},{4,0},{5,1},{6,2},{7,3},{8,12},{9,13},{10,... | collective-permute-start | bytes 76808 | tf_op jit(solution)/shard_map/ppermute | solution.py:511
  34.9 1.8 %collective-permute-start.9 = (f32[80,80]{1,0:T(8,128)S(1)}, f32[80,80]{1,0:T(8,128)S(1)}, u32[]{:S(2)}, u32[]{:S(2)}) collective-permute-start(f32[80,80]{1,0:T(8,128)S(1)} %add.7.refs_0_), channel_id=1, source_target_pairs={{0,2},{1,3},{2,0},{3,1},{4,6},{5,7},{6,4},{7,5},{8,10},{9,11},{10,... | collective-permute-start | bytes 76808 | tf_op jit(solution)/shard_map/ppermute | solution.py:511
  36.7 1.4 %collective-permute-done.11.refs_3_ = f32[80,80]{1,0:T(8,128)S(1)} collective-permute-done((f32[80,80]{1,0:T(8,128)S(1)}, f32[80,80]{1,0:T(8,128)S(1)}, u32[]{:S(2)}, u32[]{:S(2)}) %collective-permute-start.11) | collective-permute-done | bytes 25632 | tf_op jit(solution)/shard_map/ppermute | solution.py:511
  38.2 0.5 %collective-permute-done.10.refs_2_ = f32[80,80]{1,0:T(8,128)S(1)} collective-permute-done((f32[80,80]{1,0:T(8,128)S(1)}, f32[80,80]{1,0:T(8,128)S(1)}, u32[]{:S(2)}, u32[]{:S(2)}) %collective-permute-start.10) | collective-permute-done | bytes 25632 | tf_op jit(solution)/shard_map/ppermute | solution.py:511
  38.6 0.3 collective-permute-done.9.refs_1_
  38.9 0.0 copy-done.1
  38.9 0.0 copy-done.2
  38.9 5.1 %finish.1 = f32[512,256]{1,0:T(8,128)} custom-call(f32[80,80]{1,0:T(8,128)S(1)} %add.7.refs_0_, f32[80,80]{1,0:T(8,128)S(1)} %collective-permute-done.9.refs_1_, f32[80,80]{1,0:T(8,128)S(1)} %collective-permute-done.10.refs_2_, f32[80,80]{1,0:T(8,128)S(1)} %collective-permute-done.11.refs_3_, f32[8,128]{1,0:T(8,128)S(1)} %copy-done.2, ...), custom_call_target="tpu_custom_call" | custom-call | tf_op jit(solution)/shard_map/finish/pallas_call | solution.py:468
  (1 shorter events, 0.0 us)
Async XLA Ops:
  0.0 10.4 %collective-permute-start = (f32[16,2048]{1,0:T(8,128)}, f32[16,2048]{1,0:T(8,128)S(1)}, u32[]{:S(2)}, u32[]{:S(2)}) collective-permute-start(f32[16,2048]{1,0:T(8,128)} %refs_0_.1), channel_id=1, source_target_pairs={{0,1},{1,2},{2,3},{3,4},{4,5},{5,6},{6,7},{7,0},{8,9},{9,10},{10,1... | collective-permute-start | bytes 393224 | tf_op jit(solution)/shard_map/ppermute | solution.py:489
  0.5 9.9 %collective-permute-start.1 = (f32[16,2048]{1,0:T(8,128)}, f32[16,2048]{1,0:T(8,128)S(1)}, u32[]{:S(2)}, u32[]{:S(2)}) collective-permute-start(f32[16,2048]{1,0:T(8,128)} %refs_0_.1), channel_id=1, source_target_pairs={{1,0},{2,1},{3,2},{4,3},{5,4},{6,5},{7,6},{0,7},{9,8},{10,9},{11,1... | collective-permute-start | bytes 393224 | tf_op jit(solution)/shard_map/ppermute | solution.py:490
  3.4 0.9 %copy-start = (f32[16,2048]{1,0:T(8,128)S(1)}, f32[16,2048]{1,0:T(8,128)}, u32[]{:S(2)}) copy-start(f32[16,2048]{1,0:T(8,128)} %refs_0_.1) | copy-start | bytes 393220
  11.6 3.4 %collective-permute-start.3 = (f32[16,1024]{1,0:T(8,128)S(1)}, f32[16,1024]{1,0:T(8,128)S(1)}, u32[]{:S(2)}, u32[]{:S(2)}) collective-permute-start(f32[16,1024]{1,0:T(8,128)S(1)} %get-tuple-element.21.left_ref.refs_1_), channel_id=1, source_target_pairs={{1,0},{2,1},{3,2},{4,3},{5,4},{6,5},{7,6},{0,7},{9,8},{10,9},{11,1... | collective-permute-start | bytes 196616 | tf_op jit(solution)/shard_map/ppermute | solution.py:498
  12.3 5.2 %collective-permute-start.2 = (f32[16,1024]{1,0:T(8,128)S(1)}, f32[16,1024]{1,0:T(8,128)S(1)}, u32[]{:S(2)}, u32[]{:S(2)}) collective-permute-start(f32[16,1024]{1,0:T(8,128)S(1)} %get-tuple-element.22.right_ref.refs_2_), channel_id=1, source_target_pairs={{0,1},{1,2},{2,3},{3,4},{4,5},{5,6},{6,7},{7,0},{8,9},{9,10},{10,1... | collective-permute-start | bytes 196616 | tf_op jit(solution)/shard_map/ppermute | solution.py:497
  18.6 3.3 %collective-permute-start.5 = (f32[16,1024]{1,0:T(8,128)S(1)}, f32[16,1024]{1,0:T(8,128)S(1)}, u32[]{:S(2)}, u32[]{:S(2)}) collective-permute-start(f32[16,1024]{1,0:T(8,128)S(1)} %get-tuple-element.23.left_ref.refs_3_), channel_id=1, source_target_pairs={{1,0},{2,1},{3,2},{4,3},{5,4},{6,5},{7,6},{0,7},{9,8},{10,9},{11,1... | collective-permute-start | bytes 196616 | tf_op jit(solution)/shard_map/ppermute | solution.py:498
  18.9 4.6 %collective-permute-start.4 = (f32[16,1024]{1,0:T(8,128)S(1)}, f32[16,1024]{1,0:T(8,128)S(1)}, u32[]{:S(2)}, u32[]{:S(2)}) collective-permute-start(f32[16,1024]{1,0:T(8,128)S(1)} %get-tuple-element.24.right_ref.refs_4_), channel_id=1, source_target_pairs={{0,1},{1,2},{2,3},{3,4},{4,5},{5,6},{6,7},{7,0},{8,9},{9,10},{10,1... | collective-permute-start | bytes 196616 | tf_op jit(solution)/shard_map/ppermute | solution.py:497
  24.6 3.6 %collective-permute-start.7 = (f32[16,1024]{1,0:T(8,128)S(1)}, f32[16,1024]{1,0:T(8,128)S(1)}, u32[]{:S(2)}, u32[]{:S(2)}) collective-permute-start(f32[16,1024]{1,0:T(8,128)S(1)} %get-tuple-element.25.left_ref.refs_5_), channel_id=1, source_target_pairs={{1,0},{2,1},{3,2},{4,3},{5,4},{6,5},{7,6},{0,7},{9,8},{10,9},{11,1... | collective-permute-start | bytes 196616 | tf_op jit(solution)/shard_map/ppermute | solution.py:498
  25.5 13.5 %copy-start.1 = (f32[128,256]{1,0:T(8,128)S(1)}, f32[128,256]{1,0:T(8,128)}, u32[]{:S(2)}) copy-start(f32[128,256]{1,0:T(8,128)} %constant.15.clone.refs_5_) | copy-start | bytes 393220
  25.5 13.5 %copy-start.2 = (f32[8,128]{1,0:T(8,128)S(1)}, f32[8,128]{1,0:T(8,128)}, u32[]{:S(2)}) copy-start(f32[8,128]{1,0:T(8,128)} %constant.14.clone.refs_4_) | copy-start | bytes 12292
  25.5 4.6 %collective-permute-start.6 = (f32[16,1024]{1,0:T(8,128)S(1)}, f32[16,1024]{1,0:T(8,128)S(1)}, u32[]{:S(2)}, u32[]{:S(2)}) collective-permute-start(f32[16,1024]{1,0:T(8,128)S(1)} %get-tuple-element.26.right_ref.refs_6_), channel_id=1, source_target_pairs={{0,1},{1,2},{2,3},{3,4},{4,5},{5,6},{6,7},{7,0},{8,9},{9,10},{10,1... | collective-permute-start | bytes 196616 | tf_op jit(solution)/shard_map/ppermute | solution.py:497
  31.9 1.3 %collective-permute-start.8 = (f32[80,80]{1,0:T(8,128)S(1)}, f32[80,80]{1,0:T(8,128)S(1)}, u32[]{:S(2)}, u32[]{:S(2)}) collective-permute-start(f32[80,80]{1,0:T(8,128)S(1)} %get-tuple-element.27), channel_id=1, source_target_pairs={{0,1},{1,0},{2,3},{3,2},{4,5},{5,4},{6,7},{7,6},{8,9},{9,8},{10,11... | collective-permute-start | bytes 76808 | tf_op jit(solution)/shard_map/ppermute | solution.py:508
  33.2 4.9 %collective-permute-start.11 = (f32[80,80]{1,0:T(8,128)S(1)}, f32[80,80]{1,0:T(8,128)S(1)}, u32[]{:S(2)}, u32[]{:S(2)}) collective-permute-start(f32[80,80]{1,0:T(8,128)S(1)} %add.7.refs_0_), channel_id=1, source_target_pairs={{0,6},{1,7},{2,4},{3,5},{4,2},{5,3},{6,0},{7,1},{8,14},{9,15},{10,... | collective-permute-start | bytes 76808 | tf_op jit(solution)/shard_map/ppermute | solution.py:511
  34.5 4.2 %collective-permute-start.10 = (f32[80,80]{1,0:T(8,128)S(1)}, f32[80,80]{1,0:T(8,128)S(1)}, u32[]{:S(2)}, u32[]{:S(2)}) collective-permute-start(f32[80,80]{1,0:T(8,128)S(1)} %add.7.refs_0_), channel_id=1, source_target_pairs={{0,4},{1,5},{2,6},{3,7},{4,0},{5,1},{6,2},{7,3},{8,12},{9,13},{10,... | collective-permute-start | bytes 76808 | tf_op jit(solution)/shard_map/ppermute | solution.py:511
  34.9 4.0 %collective-permute-start.9 = (f32[80,80]{1,0:T(8,128)S(1)}, f32[80,80]{1,0:T(8,128)S(1)}, u32[]{:S(2)}, u32[]{:S(2)}) collective-permute-start(f32[80,80]{1,0:T(8,128)S(1)} %add.7.refs_0_), channel_id=1, source_target_pairs={{0,2},{1,3},{2,0},{3,1},{4,6},{5,7},{6,4},{7,5},{8,10},{9,11},{10,... | collective-permute-start | bytes 76808 | tf_op jit(solution)/shard_map/ppermute | solution.py:511
